TPU v7x, 32 devices: a whole 2x2x4 slice. The times are simulated.
32 devices in a mesh: group: 4 (over y, x), brick: 8 (over z, core).
Axes of the slice: x: 2, y: 2, z: 4, core: 2. Of those that a mesh axis runs over, the one named last changes fastest.
Arguments:
- populations: float32 [19, 8, 64, 128], P(None, 'group', 'brick'), may hold values from 0 to 1, as said below
- positions: float32 [3, 64, 642], P(None, ('group', 'brick')), may hold values from -6 to 6
- rest_shape: float32 [3, 642], replicated, may hold values from -6 to 6
- inverse: float32 [642, 642], replicated, may hold values from -2 to 2, as said below
- sample_cells: int32 [32, 64], P(('group', 'brick')), may hold values from 0 to 2047
- vertex_slots: int32 [32, 1284], P(('group', 'brick')), may hold values from 0 to 63, as said below
- pair_own: int32 [32, 2048], P(('group', 'brick')), may hold values from 0 to 1283
- pair_far: int32 [32, 2048], P(('group', 'brick')), may hold values from 0 to 1283
Outputs:
- new_populations: float32 [19, 8, 64, 128], P(None, 'group', 'brick')
- new_positions: float32 [3, 64, 642], P(None, ('group', 'brick'))
Inputs may be any that keep to these rules, and one draw needn't show every extreme that they name: Every population is positive and a cell's populations sum to between 0.6 and 1.4. inverse is symmetric. `vertex_slots`: on every device each slot 0 to 63 is named by at least one vertex.
All inputs are finite; a program needn't handle non-finite values.
Results may differ from a plain program's by a relative error of at most 0.0001.
Values sent between devices are 32-bit elements; how exact they have to be, the bound alone decides.
A program may use at most 64 MiB of HBM per device.

v0:
```python
import functools

import jax
import jax.numpy as jnp
from jax import lax
from jax.experimental import pallas as pl
from jax.experimental.pallas import tpu as pltpu
from jax.sharding import PartitionSpec as P

ITERS = 4
STEPS = 2


velocities = [
    (0, 0, 0),
    (0, 0, 1),
    (0, 0, -1),
    (1, 0, 0),
    (-1, 0, 0),
    (0, 1, 0),
    (0, -1, 0),
    (1, 1, 0),
    (-1, -1, 0),
    (1, -1, 0),
    (-1, 1, 0),
    (1, 0, 1),
    (-1, 0, -1),
    (1, 0, -1),
    (-1, 0, 1),
    (0, 1, 1),
    (0, -1, -1),
    (0, 1, -1),
    (0, -1, 1),
]
weights_table = [1.0 / 3.0] + [1.0 / 18.0] * 6 + [1.0 / 36.0] * 12
relax_time = 0.8
contact_gain = 0.5
contact_range = 6.0
coupling_gain = 0.05
mass_weight = 1.0
shape_weight = 1.0
time_step = 1.0


def extended(cells, sides, width):
    for axis, dim in sides:
        count = lax.axis_size(axis)
        head = lax.slice_in_dim(cells, 0, width, axis=dim)
        tail = lax.slice_in_dim(cells, cells.shape[dim] - width, cells.shape[dim], axis=dim)
        cells = jnp.concatenate(
            [
                lax.ppermute(tail, axis, [(i, (i + 1) % count) for i in range(count)]),
                cells,
                lax.ppermute(head, axis, [((i + 1) % count, i) for i in range(count)]),
            ],
            axis=dim,
        )
    return cells


def shifted_2(array, axis, by):
    peers = lax.axis_size(axis)
    return lax.ppermute(array, axis, [(i, (i + by) % peers) for i in range(peers)])


def moments(populations):
    table = jnp.array(velocities, jnp.float32)
    density = jnp.sum(populations, axis=0)
    momentum = jnp.einsum("iq,ixyz->qxyz", table, populations, precision=lax.Precision.HIGHEST)
    return (density, momentum)


def collide(populations, force):
    table = jnp.array(velocities, jnp.float32)
    weight_col = jnp.array(weights_table, jnp.float32)[:, None, None, None]
    density, momentum = moments(populations)
    veloc = (momentum + 0.5 * force) / density
    project = jnp.einsum("iq,qxyz->ixyz", table, veloc, precision=lax.Precision.HIGHEST)
    forcing = jnp.einsum("iq,qxyz->ixyz", table, force, precision=lax.Precision.HIGHEST)
    square = jnp.sum(veloc * veloc, axis=0)
    equil = weight_col * density * (1.0 + 3.0 * project + 4.5 * project * project - 1.5 * square)
    return populations - (populations - equil) / relax_time + 3.0 * weight_col * forcing


def shifted(padded, index, width_x, width_y):
    step_x, step_y, step_z = velocities[index]
    piece = padded[1 - step_x : 1 - step_x + width_x, 1 - step_y : 1 - step_y + width_y, :]
    return jnp.roll(piece, step_z, axis=2)


def stream(post):
    width_x, width_y = (post.shape[1], post.shape[2])
    padded = extended(post, (("group", 1), ("brick", 2)), 1)
    moved = [shifted(padded[index], index, width_x, width_y) for index in range(19)]
    return jnp.stack(moved, axis=0)


LANES = 128
BODY_ROWS = 4


def pieces(value):
    high = value.astype(jnp.bfloat16)
    rest = value - high.astype(jnp.float32)
    middle = rest.astype(jnp.bfloat16)
    low = (rest - middle.astype(jnp.float32)).astype(jnp.bfloat16)
    return high, middle, low


def pick(points, hot, block, body):
    rows, width = points.shape
    blocks = width // LANES
    table = jnp.concatenate([points[:, h * LANES : (h + 1) * LANES] for h in range(blocks)], axis=0)
    got = jnp.dot(jnp.concatenate(pieces(table), axis=0), hot, preferred_element_type=jnp.float32)
    size = rows * blocks
    got = got[:size] + got[size : 2 * size] + got[2 * size :]
    total = jnp.zeros((rows, hot.shape[1]), jnp.float32)
    for h in range(blocks):
        total = total + jnp.where(block == h, got[h * rows : (h + 1) * rows], 0.0)
    row_body = lax.broadcasted_iota(jnp.int32, total.shape, 0) // BODY_ROWS
    total = jnp.where(row_body == body, total, 0.0)
    out = total
    for k in range(1, rows // BODY_ROWS):
        out = out + pltpu.roll(total, k * BODY_ROWS, 0)
    return out


def bodies_kernel(
    count, verts, shape_ref, predicted_ref, rest_ref, high_ref, middle_ref, index_ref, out_ref,
    own_hot, far_hot, current, lower, send_sem, recv_sem,
):
    me = lax.axis_index("brick")
    group = lax.axis_index("group")
    above = lax.rem(me + 1, count)
    below = lax.rem(me + count - 1, count)
    barrier = pltpu.get_barrier_semaphore()
    pl.semaphore_signal(barrier, inc=1, device_id=(group, below), device_id_type=pl.DeviceIdType.MESH)
    pl.semaphore_wait(barrier, 1)
    rows, width = shape_ref.shape
    blocks = width // LANES
    bodies = rows // BODY_ROWS
    pairs = index_ref.shape[1]
    copies = []

    def send(source, slot):
        copy = pltpu.make_async_remote_copy(
            src_ref=source,
            dst_ref=lower.at[slot],
            send_sem=send_sem.at[slot],
            recv_sem=recv_sem.at[slot],
            device_id=(group, above),
            device_id_type=pl.DeviceIdType.MESH,
        )
        copy.start()
        copies.append(copy)

    send(shape_ref, 0)
    lane = lax.broadcasted_iota(jnp.int32, (LANES, pairs), 0)
    own_hot[...] = jnp.where(lane == index_ref[0:1, :], 1.0, 0.0).astype(jnp.bfloat16)
    far_hot[...] = jnp.where(lane == index_ref[3:4, :], 1.0, 0.0).astype(jnp.bfloat16)
    own_block, own_body = index_ref[1:2, :], index_ref[2:3, :]
    far_block, far_body = index_ref[4:5, :], index_ref[5:6, :]
    row_body = lax.broadcasted_iota(jnp.int32, (rows, pairs), 0) // BODY_ROWS
    for sweep in range(ITERS):
        shape = shape_ref[...] if sweep == 0 else current[sweep]
        own = pick(shape, own_hot[...], own_block, own_body)
        centroid = jnp.sum(shape, axis=1, keepdims=True) * (1.0 / verts)
        base = mass_weight * predicted_ref[...] + shape_weight * (centroid + rest_ref[...])
        copies[sweep].wait_recv()
        far = pick(lower[sweep], far_hot[...], far_block, far_body)
        diff = own - far
        square = jnp.sum(diff * diff, axis=0, keepdims=True) * (1.0 / bodies)
        push = contact_gain * jnp.exp(square * (-1.0 / contact_range)) * diff
        push = jnp.where(row_body == own_body, push, 0.0)
        parts = [
            jnp.concatenate(
                [jnp.where(own_block == h, part.astype(jnp.float32), 0.0) for h in range(blocks)], axis=0
            ).astype(jnp.bfloat16)
            for part in pieces(push)
        ]
        added = lax.dot_general(
            jnp.concatenate(parts, axis=0), own_hot[...], (((1,), (1,)), ((), ())),
            preferred_element_type=jnp.float32,
        )
        size = rows * blocks
        added = added[:size] + added[size : 2 * size] + added[2 * size :]
        contact = jnp.concatenate([added[h * rows : (h + 1) * rows] for h in range(blocks)], axis=1)
        rhs = base + contact
        split = jnp.concatenate([part.astype(jnp.float32) for part in pieces(rhs)], axis=0).astype(jnp.bfloat16)
        by_high = jnp.dot(split, high_ref[...], preferred_element_type=jnp.float32)
        by_middle = jnp.dot(split, middle_ref[...], preferred_element_type=jnp.float32)
        both = by_high + by_middle
        shape = both[:rows] + both[rows : 2 * rows] + both[2 * rows :]
        if sweep < ITERS - 1:
            current[sweep + 1] = shape
            send(current.at[sweep + 1], sweep + 1)
        else:
            out_ref[...] = shape
    for copy in copies:
        copy.wait_send()


def run_bodies(verts, shape, predicted, rest, high, middle, index):
    rows, width = shape.shape
    pairs = index.shape[1]
    return pl.pallas_call(
        functools.partial(bodies_kernel, lax.axis_size("brick"), verts),
        out_shape=jax.ShapeDtypeStruct((rows, width), jnp.float32),
        in_specs=[pl.BlockSpec(memory_space=pltpu.VMEM)] * 6,
        out_specs=pl.BlockSpec(memory_space=pltpu.VMEM),
        scratch_shapes=[
            pltpu.VMEM((LANES, pairs), jnp.bfloat16),
            pltpu.VMEM((LANES, pairs), jnp.bfloat16),
            pltpu.VMEM((ITERS, rows, width), jnp.float32),
            pltpu.VMEM((ITERS, rows, width), jnp.float32),
            pltpu.SemaphoreType.DMA((ITERS,)),
            pltpu.SemaphoreType.DMA((ITERS,)),
        ],
        compiler_params=pltpu.CompilerParams(collective_id=0, has_side_effects=True),
    )(shape, predicted, rest, high, middle, index)


def on_device(
    populations, positions, rest_shape, inverse, sample_cells, vertex_slots, pair_own, pair_far
):
    exact = lax.Precision.HIGHEST
    brick_count = lax.axis_size("brick")
    slot_count = sample_cells.shape[1]
    peer_count = slot_count // brick_count
    bodies, verts = positions.shape[1:]
    width = -(-verts // LANES) * LANES
    pad = width - verts
    grid_shape = populations.shape[1:]
    lanes = grid_shape[2]
    lines = grid_shape[0] * grid_shape[1]

    def to_rows(value):
        return jnp.pad(value.transpose(1, 0, 2), ((0, 0), (0, 1), (0, pad))).reshape(bodies * BODY_ROWS, width)

    def from_rows(value):
        return value.reshape(bodies, BODY_ROWS, width)[:, :3, :verts].transpose(1, 0, 2)

    request = sample_cells[0]
    cell_lane = (request[None, :] % lanes == jnp.arange(lanes)[:, None]).astype(jnp.float32)
    cell_line = (request[None, :] // lanes == jnp.arange(lines)[:, None]).astype(jnp.float32)
    slots = jnp.pad(vertex_slots.reshape(bodies, verts), ((0, 0), (0, pad)), constant_values=-1)
    slot_hot = (slots[:, None, :] == jnp.arange(slot_count)[None, :, None]).astype(jnp.float32)

    def places(index):
        body, vertex = index // verts, index % verts
        return [vertex % LANES, vertex // LANES, body]

    index = jnp.stack(places(pair_own[0]) + places(pair_far[0]) + [pair_own[0]] * 2, axis=0)
    full = jnp.pad(inverse, ((0, pad), (0, pad)))
    high = lax.reduce_precision(full, 8, 7)
    middle = (full - high).astype(jnp.bfloat16)
    high = high.astype(jnp.bfloat16)
    rest = to_rows(jnp.broadcast_to(rest_shape[:, None, :], positions.shape))
    dist = populations
    shape = to_rows(positions)
    for step_index in range(STEPS):
        density, momentum = moments(dist)
        flow = (momentum / density).reshape(3, lines, lanes)
        outgoing = jnp.einsum("cxl,lk->cxk", flow, cell_lane, precision=exact)
        outgoing = jnp.sum(outgoing * cell_line[None], axis=1)
        received = lax.all_to_all(
            outgoing.reshape(3, brick_count, peer_count), "brick", split_axis=1, concat_axis=1, tiled=True
        ).reshape(3, slot_count)
        received = jnp.pad(received, ((0, 1), (0, 0)))
        vertex_flow = jnp.einsum("cs,bsv->bcv", received, slot_hot, precision=exact)
        predicted = shape + time_step * vertex_flow.reshape(shape.shape)
        shape = run_bodies(verts, shape, predicted, rest, high, middle, index)
        vertex_force = (coupling_gain * (shape - predicted)).reshape(bodies, BODY_ROWS, width)
        slot_force = jnp.einsum("bcv,bsv->cs", vertex_force, slot_hot, precision=exact)[:3]
        back = lax.all_to_all(
            slot_force.reshape(3, brick_count, peer_count), "brick", split_axis=1, concat_axis=1, tiled=True
        ).reshape(3, slot_count)
        cell_force = jnp.einsum("cxk,lk->cxl", back[:, None, :] * cell_line[None], cell_lane, precision=exact)
        force = cell_force.reshape((3,) + grid_shape)
        dist = stream(collide(dist, force))
    return (dist, from_rows(shape))


def solution(mesh):
    placed = (
        P(None, "group", "brick", None),
        P(None, ("group", "brick"), None),
        P(),
        P(),
        P(("group", "brick"), None),
        P(("group", "brick"), None),
        P(("group", "brick"), None),
        P(("group", "brick"), None),
    )
    return jax.shard_map(
        on_device,
        mesh=mesh,
        in_specs=placed,
        out_specs=(P(None, "group", "brick", None), P(None, ("group", "brick"), None)),
        check_vma=False,
    )
```

profile of v0, /device:TPU:0, one launch (start us, length us, event | category | flops | bytes accessed | tf_op | source)
XLA Modules:
  0.0 111.9 jit_solution(5672477202009498648)
XLA Ops:
  0.6 0.7 fusion.49
  1.3 0.9 reduce_sum.129
  2.2 1.2 %broadcast_divide_fusion.1 = (f32[3,2,8,128]{3,0,2,1:T(4,128)S(1)}, f32[3,2,8,128]{3,0,2,1:T(4,128)S(1)}) fusion(f32[2,8,128]{2,1,0:T(8,128)S(1)} %reduce_sum.129, f32[19,3,1,1]{0,1,3,2:T(4,128)} %constant.122, f32[19,2,8,128]{3,2,1,0:T(8,128)} %param.16), kind=kOutput, calls=%fused_computation.180 | convolution fusion | flops 1406976 | bytes 213220 | tf_op jit(solution)/shard_map/iq,ixyz->qxyz/dot_general | solution.py:69
  3.7 0.6 copy.2405
  4.4 6.4 %all-to-all-start = ((f32[3,8,8]{2,0,1:T(4,128)}), f32[3,8,8]{2,0,1:T(4,128)S(1)}, u32[]{:S(2)}, u32[]{:S(2)}) async-start(f32[3,8,8]{2,0,1:T(4,128)} %copy.2405), calls=%async_computation | async-start | bytes 32768 | tf_op jit(solution)/shard_map/all_to_all | solution.py:266
  10.7 0.8 and_select_fusion
  11.8 3.3 %fusion = (bf16[768,768]{1,0:T(8,128)(2,1)}, bf16[768,768]{1,0:T(8,128)(2,1)}) fusion(f32[642,642]{1,0:T(8,128)} %param.19), kind=kLoop, calls=%fused_computation.2 | loop fusion | flops 2359296 | bytes 4007952 | tf_op jit(solution)/shard_map/convert_element_type | solution.py:256
  15.3 0.6 reshape.180.rest_ref
  15.9 0.7 stack.129.index_ref
  17.0 0.6 add.82.predicted_ref
  17.6 16.6 %shard_map.167.shape_ref = f32[8,768]{1,0:T(8,128)} custom-call(f32[8,768]{1,0:T(8,128)} %copy-done.2, f32[8,768]{1,0:T(8,128)} %add.82.predicted_ref, f32[8,768]{1,0:T(8,128)} %reshape.180.rest_ref, bf16[768,768]{1,0:T(8,128)(2,1)} %get-tuple-element.17.high_ref, bf16[768,768]{1,0:T(8,128)(2,1)} %get-tuple-element.16.middle_ref, s32[8,2048]{1,0:T(8,128)} %stack.129.index_ref), custom_call_target="tpu_custom_call" | custom-call | tf_op jit(solution)/shard_map/pallas_call | solution.py:206
  34.2 0.7 subtract_multiply_fusion.1
  35.3 8.0 %all_to_all.20 = f32[3,8,8]{2,0,1:T(4,128)S(1)} all-to-all(f32[3,8,8]{2,0,1:T(4,128)S(1)} %copy.2407), channel_id=1, replica_groups=mesh['group'=4,'brick'=8] {'brick'}, dimensions={1} | all-to-all | bytes 1536 | tf_op jit(solution)/shard_map/all_to_all | solution.py:275
  44.6 2.5 %collective-permute-start.1 = (f32[19,1,8,128]{3,0,2,1:T(8,128)S(1)}, f32[19,1,8,128]{3,0,2,1:T(8,128)S(1)}, u32[]{:S(2)}, u32[]{:S(2)}) collective-permute-start(f32[19,1,8,128]{3,0,2,1:T(8,128)S(1)} %get-tuple-element.61), channel_id=1, source_target_pairs={{8,0},{16,8},{24,16},{0,24},{9,1},{17,9},{25,17},{1,25},{10,2},{18... | collective-permute-start | bytes 233480 | tf_op jit(solution)/shard_map/ppermute | solution.py:54
  47.1 3.0 %collective-permute-done.1 = f32[19,1,8,128]{3,0,2,1:T(8,128)S(1)} collective-permute-done((f32[19,1,8,128]{3,0,2,1:T(8,128)S(1)}, f32[19,1,8,128]{3,0,2,1:T(8,128)S(1)}, u32[]{:S(2)}, u32[]{:S(2)}) %collective-permute-start.1) | collective-permute-done | bytes 77856 | tf_op jit(solution)/shard_map/ppermute | solution.py:54
  50.1 2.5 %collective-permute-done = f32[19,1,8,128]{3,0,2,1:T(8,128)S(1)} collective-permute-done((f32[19,1,8,128]{3,0,2,1:T(8,128)S(1)}, f32[19,1,8,128]{3,0,2,1:T(8,128)S(1)}, u32[]{:S(2)}, u32[]{:S(2)}) %collective-permute-start) | collective-permute-done | bytes 77856 | tf_op jit(solution)/shard_map/ppermute | solution.py:52
  53.2 1.5 %collective-permute-done.3 = f32[19,4,1,128]{3,0,2,1:T(8,128)S(1)} collective-permute-done((f32[19,4,1,128]{3,0,2,1:T(8,128)S(1)}, f32[19,4,1,128]{3,0,2,1:T(8,128)S(1)}, u32[]{:S(2)}, u32[]{:S(2)}) %collective-permute-start.3) | collective-permute-done | bytes 38944 | tf_op jit(solution)/shard_map/ppermute | solution.py:54
  54.7 3.3 %collective-permute-done.2 = f32[19,4,1,128]{3,0,2,1:T(8,128)S(1)} collective-permute-done((f32[19,4,1,128]{3,0,2,1:T(8,128)S(1)}, f32[19,4,1,128]{3,0,2,1:T(8,128)S(1)}, u32[]{:S(2)}, u32[]{:S(2)}) %collective-permute-start.2) | collective-permute-done | bytes 38944 | tf_op jit(solution)/shard_map/ppermute | solution.py:52
  61.7 8.0 %all_to_all.21 = f32[3,8,8]{2,0,1:T(4,128)S(1)} all-to-all(f32[3,8,8]{2,0,1:T(4,128)S(1)} %copy.2471), channel_id=1, replica_groups=mesh['group'=4,'brick'=8] {'brick'}, dimensions={1} | all-to-all | bytes 1536 | tf_op jit(solution)/shard_map/all_to_all | solution.py:266
  70.1 0.6 add.91.predicted_ref
  70.7 13.3 %shard_map.168 = f32[8,768]{1,0:T(8,128)} custom-call(f32[8,768]{1,0:T(8,128)} %shard_map.167.shape_ref, f32[8,768]{1,0:T(8,128)} %add.91.predicted_ref, f32[8,768]{1,0:T(8,128)} %reshape.180.rest_ref, bf16[768,768]{1,0:T(8,128)(2,1)} %get-tuple-element.17.high_ref, bf16[768,768]{1,0:T(8,128)(2,1)} %get-tuple-element.16.middle_ref, s32[8,2048]{1,0:T(8,128)} %stack.129.index_ref), custom_call_target="tpu_custom_call" | custom-call | tf_op jit(solution)/shard_map/pallas_call | solution.py:206
  84.0 0.7 subtract_multiply_fusion
  85.2 10.3 %all_to_all.22 = f32[3,8,8]{2,0,1:T(4,128)S(1)} all-to-all(f32[3,8,8]{2,0,1:T(4,128)S(1)} %copy.2473), channel_id=1, replica_groups=mesh['group'=4,'brick'=8] {'brick'}, dimensions={1} | all-to-all | bytes 1536 | tf_op jit(solution)/shard_map/all_to_all | solution.py:275
  96.6 1.1 collective-permute-start.5
  97.7 1.0 collective-permute-start.4
  98.7 0.7 reshape.191
  99.5 2.4 %collective-permute-done.5 = f32[19,1,8,128]{3,0,2,1:T(8,128)S(1)} collective-permute-done((f32[19,1,8,128]{3,0,2,1:T(8,128)S(1)}, f32[19,1,8,128]{3,0,2,1:T(8,128)S(1)}, u32[]{:S(2)}, u32[]{:S(2)}) %collective-permute-start.5) | collective-permute-done | bytes 77856 | tf_op jit(solution)/shard_map/ppermute | solution.py:54
  101.9 1.5 %collective-permute-done.4 = f32[19,1,8,128]{3,0,2,1:T(8,128)S(1)} collective-permute-done((f32[19,1,8,128]{3,0,2,1:T(8,128)S(1)}, f32[19,1,8,128]{3,0,2,1:T(8,128)S(1)}, u32[]{:S(2)}, u32[]{:S(2)}) %collective-permute-start.4) | collective-permute-done | bytes 77856 | tf_op jit(solution)/shard_map/ppermute | solution.py:52
  103.9 0.6 copy.2501
  104.5 0.8 collective-permute-done.7
  105.3 3.5 %collective-permute-done.6 = f32[19,4,1,128]{3,0,2,1:T(8,128)S(1)} collective-permute-done((f32[19,4,1,128]{3,0,2,1:T(8,128)S(1)}, f32[19,4,1,128]{3,0,2,1:T(8,128)S(1)}, u32[]{:S(2)}, u32[]{:S(2)}) %collective-permute-start.6) | collective-permute-done | bytes 38944 | tf_op jit(solution)/shard_map/ppermute | solution.py:52
  111.2 0.7 copy-done.10
  (250 shorter events, 10.7 us)
Async XLA Ops:
  4.4 12.3 %all-to-all-start = ((f32[3,8,8]{2,0,1:T(4,128)}), f32[3,8,8]{2,0,1:T(4,128)S(1)}, u32[]{:S(2)}, u32[]{:S(2)}) async-start(f32[3,8,8]{2,0,1:T(4,128)} %copy.2405), calls=%async_computation | async-start | bytes 32768 | tf_op jit(solution)/shard_map/all_to_all | solution.py:266
  11.7 3.3 %copy-start.7 = (f32[3,2,642]{2,1,0:T(2,128)S(1)}, f32[3,2,642]{2,1,0:T(2,128)}, u32[]{:S(2)}) copy-start(f32[3,2,642]{2,1,0:T(2,128)} %param.17) | copy-start | bytes 46228
  11.7 3.4 %copy-start.9 = (s32[1,1284]{1,0:T(1,128)S(1)}, s32[1,1284]{1,0:T(1,128)}, u32[]{:S(2)}) copy-start(s32[1,1284]{1,0:T(1,128)} %param.21) | copy-start | bytes 15412
  11.7 3.5 %copy-start.8 = (f32[3,642]{1,0:T(4,128)S(1)}, f32[3,642]{1,0:T(4,128)}, u32[]{:S(2)}) copy-start(f32[3,642]{1,0:T(4,128)} %param.18) | copy-start | bytes 23116
  11.8 4.2 %copy-start.5 = (s32[1,2048]{1,0:T(1,128)S(1)}, s32[1,2048]{1,0:T(1,128)}, u32[]{:S(2)}) copy-start(s32[1,2048]{1,0:T(1,128)} %param.22) | copy-start | bytes 24580
  15.1 28.7 %copy-start.6 = (f32[19,3,1,1]{0,1,3,2:T(4,128)S(1)}, f32[19,3,1,1]{0,1,3,2:T(4,128)}, u32[]{:S(2)}) copy-start(f32[19,3,1,1]{0,1,3,2:T(4,128)} %constant.122) | copy-start | bytes 688
  15.1 29.1 %copy-start = (f32[19,2,8,128]{3,2,1,0:T(8,128)S(1)}, f32[19,2,8,128]{3,2,1,0:T(8,128)}, u32[]{:S(2)}) copy-start(f32[19,2,8,128]{3,2,1,0:T(8,128)} %param.16) | copy-start | bytes 466948
  15.1 29.1 %copy-start.11 = (f32[19]{0:T(128)S(1)}, f32[19]{0:T(128)}, u32[]{:S(2)}) copy-start(f32[19]{0:T(128)} %constant.121) | copy-start | bytes 232
  15.1 29.1 %copy-start.12 = (f32[19]{0:T(128)S(1)}, f32[19]{0:T(128)}, u32[]{:S(2)}) copy-start(f32[19]{0:T(128)} %constant.102.clone) | copy-start | bytes 232
  15.2 2.4 %copy-start.2 = (f32[8,768]{1,0:T(8,128)}, f32[8,768]{1,0:T(8,128)S(1)}, u32[]{:S(2)}) copy-start(f32[8,768]{1,0:T(8,128)S(1)} %reshape.174.shape_ref) | copy-start | bytes 73732
  17.6 16.6 %copy-start.4 = (f32[8,768]{1,0:T(8,128)S(1)}, f32[8,768]{1,0:T(8,128)}, u32[]{:S(2)}) copy-start(f32[8,768]{1,0:T(8,128)} %add.82.predicted_ref) | copy-start | bytes 73732
  44.6 5.5 %collective-permute-start.1 = (f32[19,1,8,128]{3,0,2,1:T(8,128)S(1)}, f32[19,1,8,128]{3,0,2,1:T(8,128)S(1)}, u32[]{:S(2)}, u32[]{:S(2)}) collective-permute-start(f32[19,1,8,128]{3,0,2,1:T(8,128)S(1)} %get-tuple-element.61), channel_id=1, source_target_pairs={{8,0},{16,8},{24,16},{0,24},{9,1},{17,9},{25,17},{1,25},{10,2},{18... | collective-permute-start | bytes 233480 | tf_op jit(solution)/shard_map/ppermute | solution.py:54
  47.1 5.5 %collective-permute-start = (f32[19,1,8,128]{3,0,2,1:T(8,128)S(1)}, f32[19,1,8,128]{3,0,2,1:T(8,128)S(1)}, u32[]{:S(2)}, u32[]{:S(2)}) collective-permute-start(f32[19,1,8,128]{3,0,2,1:T(8,128)S(1)} %get-tuple-element.60), channel_id=1, source_target_pairs={{0,8},{8,16},{16,24},{24,0},{1,9},{9,17},{17,25},{25,1},{2,10},{10... | collective-permute-start | bytes 233480 | tf_op jit(solution)/shard_map/ppermute | solution.py:52
  52.6 2.1 %collective-permute-start.3 = (f32[19,4,1,128]{3,0,2,1:T(8,128)S(1)}, f32[19,4,1,128]{3,0,2,1:T(8,128)S(1)}, u32[]{:S(2)}, u32[]{:S(2)}) collective-permute-start(f32[19,4,1,128]{3,0,2,1:T(8,128)S(1)} %get-tuple-element.57), channel_id=1, source_target_pairs={{1,0},{2,1},{3,2},{4,3},{5,4},{6,5},{7,6},{0,7},{9,8},{10,9},{11,1... | collective-permute-start | bytes 116744 | tf_op jit(solution)/shard_map/ppermute | solution.py:54
  52.7 5.4 %collective-permute-start.2 = (f32[19,4,1,128]{3,0,2,1:T(8,128)S(1)}, f32[19,4,1,128]{3,0,2,1:T(8,128)S(1)}, u32[]{:S(2)}, u32[]{:S(2)}) collective-permute-start(f32[19,4,1,128]{3,0,2,1:T(8,128)S(1)} %get-tuple-element.56), channel_id=1, source_target_pairs={{0,1},{1,2},{2,3},{3,4},{4,5},{5,6},{6,7},{7,0},{8,9},{9,10},{10,1... | collective-permute-start | bytes 116744 | tf_op jit(solution)/shard_map/ppermute | solution.py:52
  59.2 10.9 %copy-start.1 = (f32[8,768]{1,0:T(8,128)S(1)}, f32[8,768]{1,0:T(8,128)}, u32[]{:S(2)}) copy-start(f32[8,768]{1,0:T(8,128)} %shard_map.167.shape_ref) | copy-start | bytes 73732
  70.7 13.3 %copy-start.3 = (f32[8,768]{1,0:T(8,128)S(1)}, f32[8,768]{1,0:T(8,128)}, u32[]{:S(2)}) copy-start(f32[8,768]{1,0:T(8,128)} %add.91.predicted_ref) | copy-start | bytes 73732
  96.6 5.2 %collective-permute-start.5 = (f32[19,1,8,128]{3,0,2,1:T(8,128)S(1)}, f32[19,1,8,128]{3,0,2,1:T(8,128)S(1)}, u32[]{:S(2)}, u32[]{:S(2)}) collective-permute-start(f32[19,1,8,128]{3,0,2,1:T(8,128)S(1)} %get-tuple-element.59), channel_id=1, source_target_pairs={{8,0},{16,8},{24,16},{0,24},{9,1},{17,9},{25,17},{1,25},{10,2},{18... | collective-permute-start | bytes 233480 | tf_op jit(solution)/shard_map/ppermute | solution.py:54
  97.7 5.7 %collective-permute-start.4 = (f32[19,1,8,128]{3,0,2,1:T(8,128)S(1)}, f32[19,1,8,128]{3,0,2,1:T(8,128)S(1)}, u32[]{:S(2)}, u32[]{:S(2)}) collective-permute-start(f32[19,1,8,128]{3,0,2,1:T(8,128)S(1)} %get-tuple-element.58), channel_id=1, source_target_pairs={{0,8},{8,16},{16,24},{24,0},{1,9},{9,17},{17,25},{25,1},{2,10},{10... | collective-permute-start | bytes 233480 | tf_op jit(solution)/shard_map/ppermute | solution.py:52
  103.4 1.9 %collective-permute-start.7 = (f32[19,4,1,128]{3,0,2,1:T(8,128)S(1)}, f32[19,4,1,128]{3,0,2,1:T(8,128)S(1)}, u32[]{:S(2)}, u32[]{:S(2)}) collective-permute-start(f32[19,4,1,128]{3,0,2,1:T(8,128)S(1)} %get-tuple-element.55), channel_id=1, source_target_pairs={{1,0},{2,1},{3,2},{4,3},{5,4},{6,5},{7,6},{0,7},{9,8},{10,9},{11,1... | collective-permute-start | bytes 116744 | tf_op jit(solution)/shard_map/ppermute | solution.py:54
  103.4 5.4 %collective-permute-start.6 = (f32[19,4,1,128]{3,0,2,1:T(8,128)S(1)}, f32[19,4,1,128]{3,0,2,1:T(8,128)S(1)}, u32[]{:S(2)}, u32[]{:S(2)}) collective-permute-start(f32[19,4,1,128]{3,0,2,1:T(8,128)S(1)} %get-tuple-element.54), channel_id=1, source_target_pairs={{0,1},{1,2},{2,3},{3,4},{4,5},{5,6},{6,7},{7,0},{8,9},{9,10},{10,1... | collective-permute-start | bytes 116744 | tf_op jit(solution)/shard_map/ppermute | solution.py:52
  111.2 0.7 copy-start.10
where the time goes:
time: 113 us; the launch traced here: 112 us
  Pallas kernels  29.9 us (26%)
  blocking collectives  26.3 us (23%)
  waiting for transfers between devices  18.5 us (16%)
  starting transfers between devices  12 us (11%)
  other arithmetic  10.9 us (10%)
  local copies, waits for them, and re-layouts  7.43 us (7%)
  matrix products  4.87 us (4%)
  between operations  1.93 us (2%)
    pallas_call x2, Pallas kernels, run_bodies(): pl.pallas_call(functools.partial(bodies_kernel, lax.axis_size('brick'), v...  29.9 us
    all_to_all x2, blocking collectives, on_device(): lax.all_to_all(slot_force.reshape(3, brick_count, peer_count), 'brick', s...  18.3 us
    ppermute x4, waiting for transfers between devices, extended(): lax.ppermute(tail, axis, [(i, (i + 1) % count) for i in range(count)])  10.8 us
    all_to_all x1, blocking collectives, on_device(): lax.all_to_all(outgoing.reshape(3, brick_count, peer_count), 'brick', spl...  8.02 us
    ppermute x4, waiting for transfers between devices, extended(): lax.ppermute(head, axis, [((i + 1) % count, i) for i in range(count)])  7.73 us
    all_to_all x1, starting transfers between devices, on_device(): lax.all_to_all(outgoing.reshape(3, brick_count, peer_count), 'brick', spl...  6.35 us
    ppermute x4, starting transfers between devices, extended(): lax.ppermute(head, axis, [((i + 1) % count, i) for i in range(count)])  3.67 us
    convert_element_type x1, other arithmetic, on_device(): middle = (full - high).astype(jnp.bfloat16)  3.29 us
  transfers between devices with their start and end apart: 9, of which 8 were waited for; matrix products, arithmetic and copies ran while one was open for 6% of the time, Pallas kernels for 0%

commit v1 on v0

v1 whole, which is shorter than its diff:
```python
import functools

import jax
import jax.numpy as jnp
from jax import lax
from jax.experimental import pallas as pl
from jax.experimental.pallas import tpu as pltpu
from jax.sharding import PartitionSpec as P

ITERS = 4
STEPS = 2

velocities = [
    (0, 0, 0),
    (0, 0, 1),
    (0, 0, -1),
    (1, 0, 0),
    (-1, 0, 0),
    (0, 1, 0),
    (0, -1, 0),
    (1, 1, 0),
    (-1, -1, 0),
    (1, -1, 0),
    (-1, 1, 0),
    (1, 0, 1),
    (-1, 0, -1),
    (1, 0, -1),
    (-1, 0, 1),
    (0, 1, 1),
    (0, -1, -1),
    (0, 1, -1),
    (0, -1, 1),
]
weights_table = [1.0 / 3.0] + [1.0 / 18.0] * 6 + [1.0 / 36.0] * 12
DIRS = len(velocities)
relax_time = 0.8
contact_gain = 0.5
contact_range = 6.0
coupling_gain = 0.05
mass_weight = 1.0
shape_weight = 1.0
time_step = 1.0

LANES = 128
BODY_ROWS = 4
GROUP = 32
RING = 2
MESH = pl.DeviceIdType.MESH


def up(value, unit):
    return -(-value // unit) * unit


def take(rows, index):
    return jnp.take_along_axis(rows, index, axis=1, mode="promise_in_bounds")


def halves(value):
    high = value.astype(jnp.bfloat16).astype(jnp.float32)
    return high, value - high


def signed_sum(terms, axis):
    total = None
    for p in range(1, DIRS, 2):
        sign = velocities[p][axis]
        if sign == 0:
            continue
        if total is None:
            assert sign > 0
            total = terms[p]
        else:
            total = total + terms[p] if sign > 0 else total - terms[p]
    return total


def moments(rows):
    density = functools.reduce(lambda a, b: a + b, rows)
    opposite = {p: rows[p] - rows[p + 1] for p in range(1, DIRS, 2)}
    return density, [signed_sum(opposite, axis) for axis in range(3)]


def dot_c(vector, p):
    total = None
    for axis in range(3):
        sign = velocities[p][axis]
        if sign == 0:
            continue
        if total is None:
            total = vector[axis] if sign > 0 else -vector[axis]
        else:
            total = total + vector[axis] if sign > 0 else total - vector[axis]
    return total


def collide(rows, force):
    density, momentum = moments(rows)
    inverse_density = 1.0 / density
    veloc = [(momentum[a] + 0.5 * force[a]) * inverse_density for a in range(3)]
    square = veloc[0] * veloc[0] + veloc[1] * veloc[1] + veloc[2] * veloc[2]
    keep, gain = 1.0 - 1.0 / relax_time, 1.0 / relax_time
    base = 1.0 - 1.5 * square
    scaled = [density * (gain * w) for w in (1.0 / 3.0, 1.0 / 18.0, 1.0 / 36.0)]
    out = [None] * DIRS
    out[0] = keep * rows[0] + scaled[0] * base
    for p in range(1, DIRS, 2):
        weight = weights_table[p]
        rho = scaled[1] if p < 7 else scaled[2]
        along = dot_c(veloc, p)
        even = rho * (base + 4.5 * (along * along))
        odd = rho * (3.0 * along) + (3.0 * weight) * dot_c(force, p)
        out[p] = keep * rows[p] + (even + odd)
        out[p + 1] = keep * rows[p + 1] + (even - odd)
    return out


def roll_z(value, index):
    step = velocities[index][2]
    if step == 0:
        return value
    return pltpu.roll(value, step % LANES, 1)


def step_kernel(
    sizes, pop_ref, pos_ref, rest_in, inv_hbm, cells_ref, slots_ref, own_ref, far_ref,
    outf_ref, outp_ref,
    inv_raw, inv_tail, inv_high, inv_mid, hot, mask, lhs, spread, slot_hot, deposit, row_id, turned,
    shapes, lower, rest8, slot8, slot_flat, cells_own, cells_near,
    flow_out, flow_in, force_out, force_in, blocks, edges_out, edges_in, fluid, post, fluid_2, post_2,
    field, field_2,
    inv_sem, ring_send, ring_recv, flow_send, flow_recv, force_send, force_recv,
    cells_send, cells_recv, edge_send, edge_recv, block_send, block_recv,
):
    n_brick, n_group, verts, bodies, slot_count = sizes
    me = lax.axis_index("brick")
    group = lax.axis_index("group")
    cx, cy = pop_ref.shape[1:3]
    width = shapes.shape[2]
    blocks_v = width // LANES
    rows_v = bodies * BODY_ROWS
    tiles = own_ref.shape[0]
    peer_cells = slot_count // n_brick
    wide = n_brick * GROUP
    wide_tiles = wide // LANES
    slot_tiles = cells_own.shape[1] // LANES
    long_y = cy + 2 * RING
    short_y = cy + 2
    part = cx * long_y
    f32, bf16, i32 = jnp.float32, jnp.bfloat16, jnp.int32

    def brick_at(offset):
        return lax.rem(me + (offset + n_brick), n_brick)

    def group_at(offset):
        return lax.rem(group + (offset + n_group), n_group)

    def iota(shape, axis):
        return lax.broadcasted_iota(i32, shape, axis)

    near = [(dg, o) for dg in (0, 1, -1) for o in range(n_brick) if (dg, o) != (0, 0)]
    barrier = pltpu.get_barrier_semaphore()
    for dg, o in near:
        pl.semaphore_signal(barrier, inc=1, device_id=(group_at(dg), brick_at(o)), device_id_type=MESH)
    inv_copy = pltpu.make_async_copy(inv_hbm, inv_raw, inv_sem)
    inv_copy.start()

    def remote(source, target, send, recv, dg, o):
        copy = pltpu.make_async_remote_copy(
            src_ref=source, dst_ref=target, send_sem=send, recv_sem=recv,
            device_id=(group_at(dg), brick_at(o)), device_id_type=MESH,
        )
        copy.start()
        return copy

    def all_bytes(ref, sem):
        pltpu.make_async_copy(ref, ref, sem).wait()

    shapes[0] = jnp.zeros((rows_v, width), f32)
    rest8[...] = jnp.zeros((rows_v, width), f32)
    for b in range(bodies):
        for c in range(3):
            r = b * BODY_ROWS + c
            shapes[0, r : r + 1, 0:verts] = pos_ref[c, b : b + 1, :]
            rest8[r : r + 1, 0:verts] = rest_in[c : c + 1, :]
    cells_own[...] = jnp.zeros(cells_own.shape, i32)
    cells_own[:, 0:slot_count] = cells_ref[...]
    for x in range(cx):
        for i in range(DIRS):
            edges_out[0, i, 2 * x : 2 * x + 2, :] = pop_ref[i, x, 0:RING, :]
            edges_out[1, i, 2 * x : 2 * x + 2, :] = pop_ref[i, x, cy - RING : cy, :]

    lane8 = iota((8, LANES), 1)
    sub8 = iota((8, LANES), 0)
    in_group = lane8 % GROUP
    of_group = lane8 // GROUP

    def sample(flow, step):
        lines = cx * cy
        got = []
        for t in range(slot_tiles):
            cell = cells_own[0:1, t * LANES : (t + 1) * LANES]
            at = jnp.broadcast_to(cell & (LANES - 1), (lines, LANES))
            chosen = jnp.broadcast_to(cell >> 7, (lines, LANES)) == iota((lines, LANES), 0)
            got.append([
                jnp.sum(jnp.where(chosen, take(flow[c], at), 0.0), axis=0, keepdims=True) for c in range(3)
            ])
        for base in range(0, n_brick, 8):
            start = base * peer_cells
            t, offset = start // LANES, start % LANES
            index = (offset + sub8 * peer_cells + in_group) & (LANES - 1)
            message = jnp.zeros((8, LANES), f32)
            for c in range(3):
                moved = take(jnp.broadcast_to(got[t][c], (8, LANES)), index)
                message = jnp.where(of_group == c, moved, message)
            for s in range(8):
                flow_out[step, base + s] = message[s : s + 1, :]

    def send_flow(step):
        pltpu.make_async_copy(flow_out.at[step, me], flow_in.at[step, me], flow_recv.at[step]).start()
        for o in range(1, n_brick):
            remote(
                flow_out.at[step, brick_at(o)], flow_in.at[step, me],
                flow_send.at[step], flow_recv.at[step], 0, o,
            )

    def send_ring(k):
        return remote(shapes.at[k], lower.at[k], ring_send.at[k], ring_recv.at[k], 0, 1)

    lines_own = [
        jnp.concatenate([pop_ref[i, x] for x in range(cx)], axis=0) for i in range(DIRS)
    ]
    density, momentum = moments(lines_own)
    inverse_density = 1.0 / density
    sample([m * inverse_density for m in momentum], 0)

    pl.semaphore_wait(barrier, len(near))
    send_flow(0)
    copies = [send_ring(0)]
    for n, (dg, db) in enumerate([(a, b) for a in (-1, 0, 1) for b in (-1, 0, 1) if (a, b) != (0, 0)]):
        copies.append(remote(
            cells_own, cells_near.at[1 - dg, 1 - db], cells_send.at[n], cells_recv.at[n], dg, db
        ))
    cells_copies = copies[1:]
    edge_copies = [
        remote(
            edges_out.at[side], edges_in.at[1 - dg, side],
            edge_send.at[dg + 1, side], edge_recv.at[dg + 1, side], dg, 1 if side else -1,
        )
        for dg in (0, -1, 1)
        for side in (0, 1)
    ]
    block_copies = [
        remote(pop_ref, blocks.at[n], block_send.at[n], block_recv.at[n], dg, 0)
        for n, dg in enumerate((1, -1))
    ]

    def place(index):
        body = jnp.zeros(index.shape, i32)
        for b in range(1, bodies):
            body = body + jnp.where(index >= b * verts, 1, 0)
        vertex = index - body * verts
        return vertex & (LANES - 1), vertex >> 7, body

    own_lane, own_block, own_body = place(own_ref[...])
    far_lane, far_block, far_body = place(far_ref[...])
    own_id = own_body * blocks_v + own_block
    far_id = far_body * blocks_v + far_block

    lane_square = iota((LANES, LANES), 1)
    turned[0:tiles, :] = own_lane.astype(f32)
    turned[tiles:LANES, :] = jnp.zeros((LANES - tiles, LANES), f32)
    columns = jnp.transpose(turned[...]).astype(i32)
    for t in range(tiles):
        column = jnp.broadcast_to(columns[:, t : t + 1], (LANES, LANES))
        hot[t * LANES : (t + 1) * LANES, :] = jnp.where(column == lane_square, 1.0, 0.0).astype(bf16)
        chosen = jnp.broadcast_to(own_block[t : t + 1, :], (blocks_v * rows_v, LANES))
        mask[t] = jnp.where(
            chosen == iota((blocks_v * rows_v, LANES), 0) // rows_v, 1.0, 0.0
        ).astype(bf16)
    spread[...] = jnp.zeros(spread.shape, f32)

    slot_flat[...] = jnp.zeros(slot_flat.shape, i32)
    slot_flat[:, 0 : bodies * verts] = slots_ref[...]
    flat = jnp.broadcast_to(slot_flat[...], (8, slot_flat.shape[1]))
    total = slot_flat.shape[1]
    picked = flat[:, :width]
    row_body = iota((rows_v, width), 0) // BODY_ROWS
    for b in range(1, bodies):
        moved = pltpu.roll(flat, total - b * verts, 1)[:, :width]
        picked = jnp.where(row_body == b, moved, picked)
    slot8[...] = jnp.where(iota((rows_v, width), 1) < verts, picked, -1)

    inv_copy.wait()
    chunk = 32
    full = verts // chunk
    edge = verts // LANES * LANES
    for ref in (inv_high, inv_mid):
        ref[:, edge:width] = jnp.zeros((width, width - edge), bf16)
        ref[full * chunk : width, :] = jnp.zeros((width - full * chunk, width), bf16)

    def split(n, _):
        at = pl.multiple_of(n * chunk, chunk)
        high, mid = halves(inv_raw[pl.ds(at, chunk), :])
        inv_high[pl.ds(at, chunk), 0:verts] = high.astype(bf16)
        inv_mid[pl.ds(at, chunk), 0:verts] = mid.astype(bf16)
        return 0

    lax.fori_loop(0, full, split, 0)
    if verts % chunk:
        inv_tail[...] = jnp.zeros(inv_tail.shape, f32)
        inv_tail[0 : verts % chunk, 0:verts] = inv_raw[full * chunk : verts, :]
        high, mid = halves(inv_tail[...])
        inv_high[full * chunk : (full + 1) * chunk, :] = high.astype(bf16)
        inv_mid[full * chunk : (full + 1) * chunk, :] = mid.astype(bf16)

    def pick(ref, k, lane, ident):
        total = [jnp.zeros((tiles, LANES), f32)] * 3
        for b in range(bodies):
            for h in range(blocks_v):
                chosen = ident == b * blocks_v + h
                for c in range(3):
                    r = b * BODY_ROWS + c
                    row = ref[k, r : r + 1, h * LANES : (h + 1) * LANES]
                    got = take(jnp.broadcast_to(row, (tiles, LANES)), lane)
                    total[c] = jnp.where(chosen, got, total[c])
        return total

    def contact(k, while_waiting):
        own = pick(shapes, k, own_lane, own_id)
        while_waiting()
        copies_ring[k].wait_recv()
        far = pick(lower, k, far_lane, far_id)
        diff = [a - b for a, b in zip(own, far)]
        square = diff[0] * diff[0] + diff[1] * diff[1] + diff[2] * diff[2]
        scale = contact_gain * jnp.exp(-square / contact_range)
        for b in range(bodies):
            for c in range(3):
                r = b * BODY_ROWS + c
                spread[r * tiles : (r + 1) * tiles, :] = jnp.where(own_body == b, scale * diff[c], 0.0)
        half = blocks_v * rows_v
        for t in range(tiles):
            push = spread[pl.ds(t, rows_v, stride=tiles), :]
            for n, piece in enumerate(halves(push)):
                pair = jnp.concatenate([piece, piece], axis=0).astype(bf16)
                lhs[n * half : (n + 1) * half, t * LANES : (t + 1) * LANES] = (
                    jnp.concatenate([pair] * (blocks_v // 2), axis=0) * mask[t]
                )
        added = jnp.dot(lhs[...], hot[...], preferred_element_type=f32)
        added = added[:half] + added[half:]
        return jnp.concatenate([added[h * rows_v : (h + 1) * rows_v] for h in range(blocks_v)], axis=1)

    copies_ring = {0: copies[0]}

    def received(step):
        all_bytes(flow_in.at[step], flow_recv.at[step])
        out = []
        per_tile = LANES // peer_cells
        for t in range(slot_tiles):
            index = (sub8 % BODY_ROWS) * GROUP + lane8 % peer_cells
            table = jnp.zeros((8, LANES), f32)
            for s in range(t * per_tile, min((t + 1) * per_tile, n_brick)):
                moved = take(jnp.broadcast_to(flow_in[step, s], (8, LANES)), index)
                table = jnp.where(lane8 // peer_cells == s % per_tile, moved, table)
            out.append(table)
        return out

    def vertex_flow(step):
        tables = received(step)
        parts = []
        for h in range(blocks_v):
            slot = jnp.maximum(slot8[:, h * LANES : (h + 1) * LANES], 0)
            got = take(tables[0], slot & (LANES - 1))
            for t in range(1, slot_tiles):
                got = jnp.where(slot >> 7 == t, take(tables[t], slot & (LANES - 1)), got)
            parts.append(got)
        return jnp.concatenate(parts, axis=1)

    def relax(predicted, touch, k):
        shape = shapes[k - 1]
        centroid = jnp.sum(shape, axis=1, keepdims=True) * (1.0 / verts)
        rhs = mass_weight * predicted + shape_weight * (centroid + rest8[...]) + touch
        left = jnp.concatenate(halves(rhs), axis=0).astype(bf16)
        both = jnp.dot(left, inv_high[...], preferred_element_type=f32) + jnp.dot(
            left, inv_mid[...], preferred_element_type=f32
        )
        shapes[k] = both[:rows_v] + both[rows_v:]

    def build_slots():
        column_of = []
        for h in range(blocks_v):
            rows = slot8[:, h * LANES : (h + 1) * LANES].astype(f32)
            turned[h * rows_v : (h + 1) * rows_v, :] = rows
        columns = jnp.transpose(turned[...]).astype(i32)
        for t in range(wide_tiles):
            q = iota((LANES, LANES), 1)
            brick = q // GROUP + t * (LANES // GROUP)
            inner = q % GROUP
            target = brick - 1 + inner // peer_cells
            target = jnp.where(target < 0, target + n_brick, target)
            target = jnp.where(target >= n_brick, target - n_brick, target)
            slot = jnp.where(inner < 3 * peer_cells, target * peer_cells + inner % peer_cells, -2)
            for b in range(bodies):
                for h in range(blocks_v):
                    at = h * rows_v + b * BODY_ROWS
                    column = jnp.broadcast_to(columns[:, at : at + 1], (LANES, LANES))
                    slot_hot[b, h * LANES : (h + 1) * LANES, t * LANES : (t + 1) * LANES] = jnp.where(
                        column == slot, 1.0, 0.0
                    ).astype(bf16)

    def build_deposit():
        for copy in cells_copies:
            copy.wait_recv()
        per_tile = LANES // GROUP
        for dg in range(3):
            for t in range(wide_tiles):
                start = t * per_tile * peer_cells
                source, offset = start // LANES, start % LANES
                index = offset + of_group * peer_cells + in_group % peer_cells
                side = in_group // peer_cells
                cell = jnp.zeros((8, LANES), i32)
                for db in range(3):
                    ref = cells_own if (dg, db) == (1, 1) else cells_near.at[dg, db]
                    row = ref[0:1, source * LANES : (source + 1) * LANES]
                    moved = take(jnp.broadcast_to(row, (8, LANES)), index)
                    cell = jnp.where(side == db, moved, cell)
                line = cell >> 7
                x = jnp.zeros((8, LANES), i32)
                for edge_x in range(1, cx):
                    x = x + jnp.where(line >= edge_x * cy, 1, 0)
                y = line - x * cy + cy * (side - 1) + RING
                inside = (y >= 0) & (y < long_y) & (side < 3)
                at = dg * wide_tiles + t
                row_id[dg, :, t * LANES : (t + 1) * LANES] = jnp.where(inside, x * long_y + y, -1)
                turned[at : at + 1, :] = (cell & (LANES - 1))[0:1, :].astype(f32)
        columns = jnp.transpose(turned[...]).astype(i32)
        for dg in range(3):
            for t in range(wide_tiles):
                at = dg * wide_tiles + t
                column = jnp.broadcast_to(columns[:, at : at + 1], (LANES, LANES))
                deposit[dg, t * LANES : (t + 1) * LANES, :] = jnp.where(
                    column == lane_square, 1.0, 0.0
                ).astype(bf16)

    def build_fluid():
        for copy in edge_copies + block_copies:
            copy.wait_recv()
        for i in range(DIRS):
            for dg in range(3):
                source = pop_ref if dg == 1 else blocks.at[0 if dg == 0 else 1]
                for x in range(cx):
                    at = (dg * cx + x) * long_y
                    fluid[i, at + RING : at + RING + cy, :] = source[i, x]
                    fluid[i, at + RING + cy : at + long_y, :] = edges_in[dg, 0, i, 2 * x : 2 * x + 2, :]
                    fluid[i, at : at + RING, :] = edges_in[dg, 1, i, 2 * x : 2 * x + 2, :]

    def send_force(predicted, k, step):
        change = coupling_gain * (shapes[k] - predicted)
        left = jnp.concatenate(halves(change), axis=0).astype(bf16)
        total = None
        for b in range(bodies):
            got = jnp.dot(left, slot_hot[b], preferred_element_type=f32)
            got = got[:rows_v] + got[rows_v:]
            if b:
                got = pltpu.roll(got, rows_v - b * BODY_ROWS, 0)
            total = got if total is None else total + got
        per_tile = LANES // GROUP
        index = (sub8 % per_tile) * GROUP + in_group
        for base in range(0, n_brick, 8):
            message = jnp.zeros((8, LANES), f32)
            for c in range(3):
                for n in range(8 // per_tile):
                    t = base // per_tile + n
                    row = total[c : c + 1, t * LANES : (t + 1) * LANES]
                    moved = take(jnp.broadcast_to(row, (8, LANES)), index)
                    chosen = (of_group == c) & (sub8 // per_tile == n)
                    message = jnp.where(chosen, moved, message)
            for s in range(8):
                force_out[step, base + s] = message[s : s + 1, :]
        pltpu.make_async_copy(
            force_out.at[step, me], force_in.at[step, n_brick + me], force_recv.at[step]
        ).start()
        for dg, o in near:
            remote(
                force_out.at[step, brick_at(o)], force_in.at[step, (1 - dg) * n_brick + me],
                force_send.at[step], force_recv.at[step], dg, o,
            )

    def gather_force(step):
        all_bytes(force_in.at[step], force_recv.at[step])
        per_tile = LANES // GROUP
        index = jnp.minimum(sub8, 3) * GROUP + in_group
        for dg in range(3):
            parts = []
            for t in range(wide_tiles):
                table = jnp.zeros((8, LANES), f32)
                for n in range(per_tile):
                    row = force_in[step, dg * n_brick + t * per_tile + n]
                    moved = take(jnp.broadcast_to(row, (8, LANES)), index)
                    table = jnp.where(of_group == n, moved, table)
                parts.append(table)
            table = jnp.concatenate(parts, axis=1)
            ids = jnp.broadcast_to(row_id[dg, 0:1, :], (part, wide))
            chosen = ids == iota((part, wide), 0)
            left = []
            pieces = halves(table)
            for c in range(3):
                for piece in pieces:
                    row = jnp.broadcast_to(piece[c : c + 1, :], (part, wide))
                    left.append(jnp.where(chosen, row, 0.0))
            left = jnp.concatenate(left, axis=0).astype(bf16)
            got = jnp.dot(left, deposit[dg], preferred_element_type=f32)
            for c in range(3):
                field[c, dg * part : (dg + 1) * part, :] = (
                    got[2 * c * part : (2 * c + 1) * part] + got[(2 * c + 1) * part : (2 * c + 2) * part]
                )

    def nothing():
        pass

    background = {0: nothing, 1: build_slots, 2: build_deposit, 3: build_fluid}
    k = 0
    for step in range(STEPS):
        touch = contact(k, background.get(k, nothing))
        predicted = shapes[k] + time_step * vertex_flow(step)
        for sweep in range(ITERS):
            k += 1
            relax(predicted, touch, k)
            if sweep < ITERS - 1:
                copies_ring[k] = send_ring(k)
                touch = contact(k, background.get(k, nothing))
        send_force(predicted, k, step)
        if step < STEPS - 1:
            copies_ring[k] = send_ring(k)
            gather_force(step)
            for q in range(3 * part // 8):
                rows = slice(8 * q, 8 * q + 8)
                after = collide([fluid[i, rows, :] for i in range(DIRS)], [field[c, rows, :] for c in range(3)])
                for i in range(DIRS):
                    post[i, rows, :] = roll_z(after[i], i)
            for i in range(DIRS):
                step_x, step_y, _ = velocities[i]
                for x in range(cx + 2):
                    at = (x + 1 - step_x) * long_y + 1 - step_y
                    fluid_2[i, x * short_y : (x + 1) * short_y, :] = post[i, at : at + short_y, :]
            lines_own = [
                jnp.concatenate(
                    [fluid_2[i, (x + 1) * short_y + 1 : (x + 1) * short_y + 1 + cy, :] for x in range(cx)], axis=0
                )
                for i in range(DIRS)
            ]
            density, momentum = moments(lines_own)
            inverse_density = 1.0 / density
            sample([m * inverse_density for m in momentum], step + 1)
            send_flow(step + 1)

    for b in range(bodies):
        for c in range(3):
            r = b * BODY_ROWS + c
            outp_ref[c, b : b + 1, :] = shapes[k, r : r + 1, 0:verts]
    gather_force(STEPS - 1)
    for c in range(3):
        for x in range(cx + 2):
            at = (x + 1) * long_y + 1
            field_2[c, x * short_y : (x + 1) * short_y, :] = field[c, at : at + short_y, :]
    for q in range((cx + 2) * short_y // 8):
        rows = slice(8 * q, 8 * q + 8)
        after = collide([fluid_2[i, rows, :] for i in range(DIRS)], [field_2[c, rows, :] for c in range(3)])
        for i in range(DIRS):
            post_2[i, rows, :] = roll_z(after[i], i)
    for i in range(DIRS):
        step_x, step_y, _ = velocities[i]
        for x in range(cx):
            at = (x + 1 - step_x) * short_y + 1 - step_y
            outf_ref[i, x] = post_2[i, at : at + cy, :]

    for copy in copies_ring.values():
        copy.wait_send()
    for copy in cells_copies + edge_copies + block_copies:
        copy.wait_send()
    for step in range(STEPS):
        all_bytes(flow_out.at[step, pl.ds(0, n_brick - 1)], flow_send.at[step])
        all_bytes(force_in.at[step, pl.ds(0, 3 * n_brick - 1)], force_send.at[step])


def on_device(
    populations, positions, rest_shape, inverse, sample_cells, vertex_slots, pair_own, pair_far
):
    n_brick = lax.axis_size("brick")
    n_group = lax.axis_size("group")
    slot_count = sample_cells.shape[1]
    bodies, verts = positions.shape[1:]
    width = up(verts, LANES)
    rows = bodies * BODY_ROWS
    dirs, cx, cy, lanes = populations.shape
    tiles = pair_own.shape[1] // LANES
    wide = n_brick * GROUP
    long_rows = 3 * cx * (cy + 2 * RING)
    short_rows = (cx + 2) * (cy + 2)
    sweeps = STEPS * ITERS
    blocks_v = width // LANES
    f32, bf16, i32 = jnp.float32, jnp.bfloat16, jnp.int32
    vmem = pltpu.VMEM
    dma = pltpu.SemaphoreType.DMA
    in_vmem = pl.BlockSpec(memory_space=pltpu.VMEM)
    return pl.pallas_call(
        functools.partial(step_kernel, (n_brick, n_group, verts, bodies, slot_count)),
        out_shape=(
            jax.ShapeDtypeStruct(populations.shape, f32),
            jax.ShapeDtypeStruct(positions.shape, f32),
        ),
        in_specs=[in_vmem, in_vmem, in_vmem, pl.BlockSpec(memory_space=pl.ANY)] + [in_vmem] * 4,
        out_specs=(in_vmem, in_vmem),
        scratch_shapes=[
            vmem((verts, verts), f32),
            vmem((32, width), f32),
            vmem((width, width), bf16),
            vmem((width, width), bf16),
            vmem((tiles * LANES, LANES), bf16),
            vmem((tiles, blocks_v * rows, LANES), bf16),
            vmem((2 * blocks_v * rows, tiles * LANES), bf16),
            vmem((rows * tiles, LANES), f32),
            vmem((bodies, width, wide), bf16),
            vmem((3, wide, LANES), bf16),
            vmem((3, 8, wide), i32),
            vmem((LANES, LANES), f32),
            vmem((sweeps + 1, rows, width), f32),
            vmem((sweeps, rows, width), f32),
            vmem((rows, width), f32),
            vmem((rows, width), i32),
            vmem((1, up(bodies * verts + width, LANES)), i32),
            vmem((1, up(slot_count, LANES)), i32),
            vmem((3, 3, 1, up(slot_count, LANES)), i32),
            vmem((STEPS, n_brick, 1, LANES), f32),
            vmem((STEPS, n_brick, 1, LANES), f32),
            vmem((STEPS, n_brick, 1, LANES), f32),
            vmem((STEPS, 3 * n_brick, 1, LANES), f32),
            vmem((2,) + populations.shape, f32),
            vmem((2, dirs, 2 * cx, LANES), f32),
            vmem((3, 2, dirs, 2 * cx, LANES), f32),
            vmem((dirs, long_rows, LANES), f32),
            vmem((dirs, long_rows, LANES), f32),
            vmem((dirs, short_rows, LANES), f32),
            vmem((dirs, short_rows, LANES), f32),
            vmem((3, long_rows, LANES), f32),
            vmem((3, short_rows, LANES), f32),
            dma,
            dma((sweeps,)),
            dma((sweeps,)),
            dma((STEPS,)),
            dma((STEPS,)),
            dma((STEPS,)),
            dma((STEPS,)),
            dma((8,)),
            dma((8,)),
            dma((3, 2)),
            dma((3, 2)),
            dma((2,)),
            dma((2,)),
        ],
        compiler_params=pltpu.CompilerParams(
            collective_id=0, has_side_effects=True, vmem_limit_bytes=60 * 1024 * 1024
        ),
    )(
        populations, positions, rest_shape, inverse, sample_cells, vertex_slots,
        pair_own.reshape(tiles, LANES), pair_far.reshape(tiles, LANES),
    )


def solution(mesh):
    placed = (
        P(None, "group", "brick", None),
        P(None, ("group", "brick"), None),
        P(),
        P(),
        P(("group", "brick"), None),
        P(("group", "brick"), None),
        P(("group", "brick"), None),
        P(("group", "brick"), None),
    )
    return jax.shard_map(
        on_device,
        mesh=mesh,
        in_specs=placed,
        out_specs=(P(None, "group", "brick", None), P(None, ("group", "brick"), None)),
        check_vma=False,
    )
```

time: 113 us -> 48.4 us (0.43)
  blocking collectives: 26.3 us -> 0 us
  waiting for transfers between devices: 18.5 us -> 0 us
  Pallas kernels: 29.9 us -> 44.6 us
  starting transfers between devices: 12 us -> 0 us
  other arithmetic: 10.9 us -> 0 us
  matrix products: 4.87 us -> 0 us
  local copies, waits for them, and re-layouts: 7.43 us -> 2.92 us
  between operations: 1.93 us -> 0.64 us
    all_to_all x3 -> x0, blocking collectives: 26.3 us -> none  [the longest x2 18.3 us: on_device(): lax.all_to_all(slot_force.reshape(3, brick_count, peer_count), 'brick', s...]
    ppermute x8 -> x0, waiting for transfers between devices: 18.5 us -> none  [the longest x4 10.8 us: extended(): lax.ppermute(tail, axis, [(i, (i + 1) % count) for i in range(count)])]
    pallas_call x2 -> x1, Pallas kernels: 29.9 us -> 44.6 us  [on_device(): pl.pallas_call(functools.partial(step_kernel, (n_brick, n_group, verts, b...]
    all_to_all x1 -> x0, starting transfers between devices: 6.35 us -> none  [on_device(): lax.all_to_all(outgoing.reshape(3, brick_count, peer_count), 'brick', spl...]
    ppermute x8 -> x0, starting transfers between devices: 5.69 us -> none  [the longest x4 3.67 us: extended(): lax.ppermute(head, axis, [((i + 1) % count, i) for i in range(count)])]
    dot_general x14 -> x0, matrix products: 4.87 us -> none  [the longest x2 1.41 us: moments(): jnp.einsum('iq,ixyz->qxyz', table, populations, precision=lax.Precision.H...]
    convert_element_type x2 -> x0, other arithmetic: 3.3 us -> none  [the longest x1 3.29 us: on_device(): middle = (full - high).astype(jnp.bfloat16)]
    reshape x18 -> x0, local copies, waits for them, and re-layouts: 2.63 us -> none  [the longest x4 0.79 us: on_device(): outgoing.reshape(3, brick_count, peer_count)]
  transfers between devices with their start and end apart: 9 -> 0, of which waited for: 8 -> 0; matrix products, arithmetic and copies ran while one was open for 6% -> 0% of each run, Pallas kernels for 0% -> 0%
where the time goes in v1:
time: 48.4 us; the launch traced here: 48.2 us
  Pallas kernels  44.6 us (92%)
  local copies, waits for them, and re-layouts  2.92 us (6%)
  between operations  0.64 us (1%)
    pallas_call x1, Pallas kernels, on_device(): pl.pallas_call(functools.partial(step_kernel, (n_brick, n_group, verts, b...  44.6 us
    unnamed x2, local copies, waits for them, and re-layouts  2.92 us

profile of v1, /device:TPU:0, one launch (start us, length us, event | category | flops | bytes accessed | tf_op | source)
XLA Modules:
  0.0 48.2 jit_solution(1259718613907134176)
XLA Ops:
  0.6 44.6 %shard_map.95 = (f32[19,2,8,128]{3,2,1,0:T(8,128)}, f32[3,2,642]{2,1,0:T(2,128)}) custom-call(f32[19,2,8,128]{3,2,1,0:T(8,128)} %pop_ref.1, f32[3,2,642]{2,1,0:T(2,128)} %pos_ref.1, f32[3,642]{1,0:T(4,128)} %rest_in.1, f32[642,642]{1,0:T(8,128)} %inv_hbm.1, s32[1,64]{1,0:T(1,128)} %cells_ref.1, s32[1,1284]{1,0:T(1,128)} %slots_ref.1, s32[16,128]{1,0:T(8,128)} %bitcast.2, ...), custom_call_target="tpu_custom_call" | custom-call | tf_op jit(solution)/shard_map/pallas_call | solution.py:606
  45.3 1.6 %copy.12 = f32[19,2,8,128]{3,2,1,0:T(8,128)} copy(f32[19,2,8,128]{3,2,1,0:T(8,128)} %get-tuple-element.4) | data formatting | bytes 311296
  46.9 1.3 %copy.13 = f32[3,2,642]{2,1,0:T(2,128)} copy(f32[3,2,642]{2,1,0:T(2,128)} %get-tuple-element.5) | data formatting | bytes 30816

commit v2 on v1

--- a/solution.py
+++ b/solution.py
@@ -123,13 +123,15 @@
 
 
 def step_kernel(
-    sizes, pop_ref, pos_ref, rest_in, inv_hbm, cells_ref, slots_ref, own_ref, far_ref,
+    sizes, pop_hbm, pos_hbm, rest_hbm, inv_hbm, cells_hbm, slots_hbm, own_hbm, far_hbm,
     outf_ref, outp_ref,
-    inv_raw, inv_tail, inv_high, inv_mid, hot, mask, lhs, spread, slot_hot, deposit, row_id, turned,
-    shapes, lower, rest8, slot8, slot_flat, cells_own, cells_near,
+    pop_ref, pos_ref, rest_in, cells_ref, slots_ref, pairs,
+    inv_raw, inv_tail, inv_high, inv_mid, places, hot, mask, lhs, spread, slot_hot, deposit, row_id, turned,
+    shapes, lower, shapes_near, pairs_near, slots_near, ghosts, predicted_of,
+    rest8, slot8, slot_flat, cells_own, cells_near,
     flow_out, flow_in, force_out, force_in, blocks, edges_out, edges_in, fluid, post, fluid_2, post_2,
     field, field_2,
-    inv_sem, ring_send, ring_recv, flow_send, flow_recv, force_send, force_recv,
+    in_sem, ready, ring_send, ring_recv, near_send, near_recv, pairs_send, pairs_recv, slots_send, slots_recv, flow_send, flow_recv, force_send, force_recv,
     cells_send, cells_recv, edge_send, edge_recv, block_send, block_recv,
 ):
     n_brick, n_group, verts, bodies, slot_count = sizes
@@ -139,7 +141,8 @@
     width = shapes.shape[2]
     blocks_v = width // LANES
     rows_v = bodies * BODY_ROWS
-    tiles = own_ref.shape[0]
+    tiles = pairs.shape[1]
+    depth = ITERS
     peer_cells = slot_count // n_brick
     wide = n_brick * GROUP
     wide_tiles = wide // LANES
@@ -159,11 +162,22 @@
         return lax.broadcasted_iota(i32, shape, axis)
 
     near = [(dg, o) for dg in (0, 1, -1) for o in range(n_brick) if (dg, o) != (0, 0)]
+    first = [(0, o) for o in range(1, n_brick)] + [(1, 0), (-1, 0)]
     barrier = pltpu.get_barrier_semaphore()
-    for dg, o in near:
+    for dg, o in first:
         pl.semaphore_signal(barrier, inc=1, device_id=(group_at(dg), brick_at(o)), device_id_type=MESH)
-    inv_copy = pltpu.make_async_copy(inv_hbm, inv_raw, inv_sem)
-    inv_copy.start()
+    loads = [
+        pltpu.make_async_copy(source, target, in_sem.at[n])
+        for n, (source, target) in enumerate([
+            (pop_hbm, pop_ref), (cells_hbm, cells_ref), (pos_hbm, pos_ref), (rest_hbm, rest_in),
+            (own_hbm, pairs.at[0]), (far_hbm, pairs.at[1]), (slots_hbm, slots_ref), (inv_hbm, inv_raw),
+        ])
+    ]
+    for load in loads:
+        load.start()
+    inv_copy = loads.pop()
+    for load in loads:
+        load.wait()
 
     def remote(source, target, send, recv, dg, o):
         copy = pltpu.make_async_remote_copy(
@@ -206,13 +220,15 @@
                 jnp.sum(jnp.where(chosen, take(flow[c], at), 0.0), axis=0, keepdims=True) for c in range(3)
             ])
         for base in range(0, n_brick, 8):
-            start = base * peer_cells
-            t, offset = start // LANES, start % LANES
-            index = (offset + sub8 * peer_cells + in_group) & (LANES - 1)
+            owner = base + sub8 - in_group // peer_cells
+            owner = jnp.where(owner < 0, owner + n_brick, owner)
+            slot = owner * peer_cells + in_group % peer_cells
+            touched = {(base + n) % n_brick * peer_cells // LANES for n in range(1 - depth, 8)}
             message = jnp.zeros((8, LANES), f32)
             for c in range(3):
-                moved = take(jnp.broadcast_to(got[t][c], (8, LANES)), index)
-                message = jnp.where(of_group == c, moved, message)
+                for t in sorted(touched):
+                    moved = take(jnp.broadcast_to(got[t][c], (8, LANES)), slot & (LANES - 1))
+                    message = jnp.where((of_group == c) & (slot >> 7 == t), moved, message)
             for s in range(8):
                 flow_out[step, base + s] = message[s : s + 1, :]
 
@@ -234,9 +250,12 @@
     inverse_density = 1.0 / density
     sample([m * inverse_density for m in momentum], 0)
 
-    pl.semaphore_wait(barrier, len(near))
+    pl.semaphore_wait(barrier, len(first))
+    for dg in (1, -1):
+        pl.semaphore_signal(ready, inc=1, device_id=(group_at(dg), brick_at(0)), device_id_type=MESH)
     send_flow(0)
     copies = [send_ring(0)]
+    pl.semaphore_wait(ready, 2)
     for n, (dg, db) in enumerate([(a, b) for a in (-1, 0, 1) for b in (-1, 0, 1) if (a, b) != (0, 0)]):
         copies.append(remote(
             cells_own, cells_near.at[1 - dg, 1 - db], cells_send.at[n], cells_recv.at[n], dg, db
@@ -255,6 +274,15 @@
         for n, dg in enumerate((1, -1))
     ]
 
+    ghost_copies = []
+    for e in range(1, depth):
+        ghost_copies.append(remote(
+            pairs, pairs_near.at[e - 1], pairs_send.at[e - 1], pairs_recv.at[e - 1], 0, e
+        ))
+        ghost_copies.append(remote(
+            slots_ref, slots_near.at[e - 1], slots_send.at[e - 1], slots_recv.at[e - 1], 0, e
+        ))
+
     def place(index):
         body = jnp.zeros(index.shape, i32)
         for b in range(1, bodies):
@@ -262,34 +290,48 @@
         vertex = index - body * verts
         return vertex & (LANES - 1), vertex >> 7, body
 
-    own_lane, own_block, own_body = place(own_ref[...])
-    far_lane, far_block, far_body = place(far_ref[...])
-    own_id = own_body * blocks_v + own_block
-    far_id = far_body * blocks_v + far_block
-
     lane_square = iota((LANES, LANES), 1)
-    turned[0:tiles, :] = own_lane.astype(f32)
-    turned[tiles:LANES, :] = jnp.zeros((LANES - tiles, LANES), f32)
-    columns = jnp.transpose(turned[...]).astype(i32)
-    for t in range(tiles):
-        column = jnp.broadcast_to(columns[:, t : t + 1], (LANES, LANES))
-        hot[t * LANES : (t + 1) * LANES, :] = jnp.where(column == lane_square, 1.0, 0.0).astype(bf16)
-        chosen = jnp.broadcast_to(own_block[t : t + 1, :], (blocks_v * rows_v, LANES))
-        mask[t] = jnp.where(
-            chosen == iota((blocks_v * rows_v, LANES), 0) // rows_v, 1.0, 0.0
-        ).astype(bf16)
+
+    def build_pairs(e, ref):
+        own_lane, own_block, own_body = place(ref[0])
+        far_lane, far_block, far_body = place(ref[1])
+        places[e, 0] = own_lane
+        places[e, 1] = own_body * blocks_v + own_block
+        places[e, 2] = far_lane
+        places[e, 3] = far_body * blocks_v + far_block
+        turned[e, 0:tiles, :] = own_lane.astype(f32)
+        turned[e, tiles:LANES, :] = jnp.zeros((LANES - tiles, LANES), f32)
+        columns = jnp.transpose(turned[e]).astype(i32)
+        for t in range(tiles):
+            column = jnp.broadcast_to(columns[:, t : t + 1], (LANES, LANES))
+            hot[e, t * LANES : (t + 1) * LANES, :] = jnp.where(column == lane_square, 1.0, 0.0).astype(bf16)
+            chosen = jnp.broadcast_to(own_block[t : t + 1, :], (blocks_v * rows_v, LANES))
+            mask[e, t] = jnp.where(
+                chosen == iota((blocks_v * rows_v, LANES), 0) // rows_v, 1.0, 0.0
+            ).astype(bf16)
+
+    def place_slots(e, ref):
+        slot_flat[e, :, 0 : bodies * verts] = ref[...]
+        total = slot_flat.shape[2]
+        flat = jnp.broadcast_to(slot_flat[e], (8, total))
+        picked = flat[:, :width]
+        row_body = iota((rows_v, width), 0) // BODY_ROWS
+        for b in range(1, bodies):
+            moved = pltpu.roll(flat, total - b * verts, 1)[:, :width]
+            picked = jnp.where(row_body == b, moved, picked)
+        slot8[e] = jnp.where(iota((rows_v, width), 1) < verts, picked, -1)
+
+    slot_flat[...] = jnp.zeros(slot_flat.shape, i32)
     spread[...] = jnp.zeros(spread.shape, f32)
-
-    slot_flat[...] = jnp.zeros(slot_flat.shape, i32)
-    slot_flat[:, 0 : bodies * verts] = slots_ref[...]
-    flat = jnp.broadcast_to(slot_flat[...], (8, slot_flat.shape[1]))
-    total = slot_flat.shape[1]
-    picked = flat[:, :width]
-    row_body = iota((rows_v, width), 0) // BODY_ROWS
-    for b in range(1, bodies):
-        moved = pltpu.roll(flat, total - b * verts, 1)[:, :width]
-        picked = jnp.where(row_body == b, moved, picked)
-    slot8[...] = jnp.where(iota((rows_v, width), 1) < verts, picked, -1)
+    build_pairs(0, pairs)
+    place_slots(0, slots_ref)
+
+    def build_ghosts():
+        for copy in ghost_copies:
+            copy.wait_recv()
+        for e in range(1, depth):
+            build_pairs(e, pairs_near.at[e - 1])
+            place_slots(e, slots_near.at[e - 1])
 
     inv_copy.wait()
     chunk = 32
@@ -314,50 +356,52 @@
         inv_high[full * chunk : (full + 1) * chunk, :] = high.astype(bf16)
         inv_mid[full * chunk : (full + 1) * chunk, :] = mid.astype(bf16)
 
-    def pick(ref, k, lane, ident):
+    def pick(ref, lane, ident):
         total = [jnp.zeros((tiles, LANES), f32)] * 3
         for b in range(bodies):
             for h in range(blocks_v):
                 chosen = ident == b * blocks_v + h
                 for c in range(3):
                     r = b * BODY_ROWS + c
-                    row = ref[k, r : r + 1, h * LANES : (h + 1) * LANES]
+                    row = ref[r : r + 1, h * LANES : (h + 1) * LANES]
                     got = take(jnp.broadcast_to(row, (tiles, LANES)), lane)
                     total[c] = jnp.where(chosen, got, total[c])
         return total
 
-    def contact(k, while_waiting):
-        own = pick(shapes, k, own_lane, own_id)
-        while_waiting()
-        copies_ring[k].wait_recv()
-        far = pick(lower, k, far_lane, far_id)
+    def contact(e, shape_of, lower_of, before_far):
+        own_id = places[e, 1]
+        own = pick(shape_of, places[e, 0], own_id)
+        before_far()
+        far = pick(lower_of, places[e, 2], places[e, 3])
         diff = [a - b for a, b in zip(own, far)]
         square = diff[0] * diff[0] + diff[1] * diff[1] + diff[2] * diff[2]
         scale = contact_gain * jnp.exp(-square / contact_range)
         for b in range(bodies):
+            inside = (own_id >= b * blocks_v) & (own_id < (b + 1) * blocks_v)
             for c in range(3):
                 r = b * BODY_ROWS + c
-                spread[r * tiles : (r + 1) * tiles, :] = jnp.where(own_body == b, scale * diff[c], 0.0)
+                spread[e, r * tiles : (r + 1) * tiles, :] = jnp.where(inside, scale * diff[c], 0.0)
         half = blocks_v * rows_v
         for t in range(tiles):
-            push = spread[pl.ds(t, rows_v, stride=tiles), :]
+            push = spread[e, pl.ds(t, rows_v, stride=tiles), :]
             for n, piece in enumerate(halves(push)):
                 pair = jnp.concatenate([piece, piece], axis=0).astype(bf16)
-                lhs[n * half : (n + 1) * half, t * LANES : (t + 1) * LANES] = (
-                    jnp.concatenate([pair] * (blocks_v // 2), axis=0) * mask[t]
+                lhs[e, n * half : (n + 1) * half, t * LANES : (t + 1) * LANES] = (
+                    jnp.concatenate([pair] * (blocks_v // 2), axis=0) * mask[e, t]
                 )
-        added = jnp.dot(lhs[...], hot[...], preferred_element_type=f32)
+        middle = tiles // 2 * LANES
+        added = jnp.dot(lhs[e, :, :middle], hot[e, :middle], preferred_element_type=f32)
+        added = added + jnp.dot(lhs[e, :, middle:], hot[e, middle:], preferred_element_type=f32)
         added = added[:half] + added[half:]
         return jnp.concatenate([added[h * rows_v : (h + 1) * rows_v] for h in range(blocks_v)], axis=1)
 
     copies_ring = {0: copies[0]}
 
-    def received(step):
-        all_bytes(flow_in.at[step], flow_recv.at[step])
+    def received(step, e):
         out = []
         per_tile = LANES // peer_cells
         for t in range(slot_tiles):
-            index = (sub8 % BODY_ROWS) * GROUP + lane8 % peer_cells
+            index = (sub8 % BODY_ROWS) * GROUP + e * peer_cells + lane8 % peer_cells
             table = jnp.zeros((8, LANES), f32)
             for s in range(t * per_tile, min((t + 1) * per_tile, n_brick)):
                 moved = take(jnp.broadcast_to(flow_in[step, s], (8, LANES)), index)
@@ -365,33 +409,42 @@
             out.append(table)
         return out
 
-    def vertex_flow(step):
-        tables = received(step)
+    def vertex_flow(step, e):
+        tables = received(step, e)
         parts = []
         for h in range(blocks_v):
-            slot = jnp.maximum(slot8[:, h * LANES : (h + 1) * LANES], 0)
+            slot = jnp.maximum(slot8[e, :, h * LANES : (h + 1) * LANES], 0)
             got = take(tables[0], slot & (LANES - 1))
             for t in range(1, slot_tiles):
                 got = jnp.where(slot >> 7 == t, take(tables[t], slot & (LANES - 1)), got)
             parts.append(got)
         return jnp.concatenate(parts, axis=1)
 
-    def relax(predicted, touch, k):
-        shape = shapes[k - 1]
-        centroid = jnp.sum(shape, axis=1, keepdims=True) * (1.0 / verts)
-        rhs = mass_weight * predicted + shape_weight * (centroid + rest8[...]) + touch
-        left = jnp.concatenate(halves(rhs), axis=0).astype(bf16)
-        both = jnp.dot(left, inv_high[...], preferred_element_type=f32) + jnp.dot(
-            left, inv_mid[...], preferred_element_type=f32
-        )
-        shapes[k] = both[:rows_v] + both[rows_v:]
+    def relax(cases):
+        high, mid = [], []
+        for shape, predicted, touch in cases:
+            centroid = jnp.sum(shape, axis=1, keepdims=True) * (1.0 / verts)
+            rhs = mass_weight * predicted + shape_weight * (centroid + rest8[...]) + touch
+            a, b = halves(rhs)
+            high.append(a)
+            mid.append(b)
+        if len(cases) % 2:
+            high.append(jnp.zeros((rows_v, width), f32))
+            mid.append(jnp.zeros((rows_v, width), f32))
+        count = len(high) * rows_v
+        high = jnp.concatenate(high, axis=0).astype(bf16)
+        left = jnp.concatenate([high, jnp.concatenate(mid, axis=0).astype(bf16)], axis=0)
+        both = jnp.dot(left, inv_high[...], preferred_element_type=f32)
+        rest = jnp.dot(high, inv_mid[...], preferred_element_type=f32)
+        both = both[:count] + both[count:] + rest
+        return [both[n * rows_v : (n + 1) * rows_v] for n in range(len(cases))]
 
     def build_slots():
         column_of = []
         for h in range(blocks_v):
-            rows = slot8[:, h * LANES : (h + 1) * LANES].astype(f32)
-            turned[h * rows_v : (h + 1) * rows_v, :] = rows
-        columns = jnp.transpose(turned[...]).astype(i32)
+            rows = slot8[0, :, h * LANES : (h + 1) * LANES].astype(f32)
+            turned[0, h * rows_v : (h + 1) * rows_v, :] = rows
+        columns = jnp.transpose(turned[0]).astype(i32)
         for t in range(wide_tiles):
             q = iota((LANES, LANES), 1)
             brick = q // GROUP + t * (LANES // GROUP)
@@ -432,8 +485,8 @@
                 inside = (y >= 0) & (y < long_y) & (side < 3)
                 at = dg * wide_tiles + t
                 row_id[dg, :, t * LANES : (t + 1) * LANES] = jnp.where(inside, x * long_y + y, -1)
-                turned[at : at + 1, :] = (cell & (LANES - 1))[0:1, :].astype(f32)
-        columns = jnp.transpose(turned[...]).astype(i32)
+                turned[1, at : at + 1, :] = (cell & (LANES - 1))[0:1, :].astype(f32)
+        columns = jnp.transpose(turned[1]).astype(i32)
         for dg in range(3):
             for t in range(wide_tiles):
                 at = dg * wide_tiles + t
@@ -454,8 +507,8 @@
                     fluid[i, at + RING + cy : at + long_y, :] = edges_in[dg, 0, i, 2 * x : 2 * x + 2, :]
                     fluid[i, at : at + RING, :] = edges_in[dg, 1, i, 2 * x : 2 * x + 2, :]
 
-    def send_force(predicted, k, step):
-        change = coupling_gain * (shapes[k] - predicted)
+    def send_force(predicted, shape, step):
+        change = coupling_gain * (shape - predicted)
         left = jnp.concatenate(halves(change), axis=0).astype(bf16)
         total = None
         for b in range(bodies):
@@ -518,47 +571,73 @@
     def nothing():
         pass
 
-    background = {0: nothing, 1: build_slots, 2: build_deposit, 3: build_fluid}
-    k = 0
-    for step in range(STEPS):
-        touch = contact(k, background.get(k, nothing))
-        predicted = shapes[k] + time_step * vertex_flow(step)
-        for sweep in range(ITERS):
-            k += 1
-            relax(predicted, touch, k)
-            if sweep < ITERS - 1:
-                copies_ring[k] = send_ring(k)
-                touch = contact(k, background.get(k, nothing))
-        send_force(predicted, k, step)
-        if step < STEPS - 1:
-            copies_ring[k] = send_ring(k)
-            gather_force(step)
-            for q in range(3 * part // 8):
-                rows = slice(8 * q, 8 * q + 8)
-                after = collide([fluid[i, rows, :] for i in range(DIRS)], [field[c, rows, :] for c in range(3)])
-                for i in range(DIRS):
-                    post[i, rows, :] = roll_z(after[i], i)
-            for i in range(DIRS):
-                step_x, step_y, _ = velocities[i]
-                for x in range(cx + 2):
-                    at = (x + 1 - step_x) * long_y + 1 - step_y
-                    fluid_2[i, x * short_y : (x + 1) * short_y, :] = post[i, at : at + short_y, :]
-            lines_own = [
-                jnp.concatenate(
-                    [fluid_2[i, (x + 1) * short_y + 1 : (x + 1) * short_y + 1 + cy, :] for x in range(cx)], axis=0
-                )
-                for i in range(DIRS)
-            ]
-            density, momentum = moments(lines_own)
-            inverse_density = 1.0 / density
-            sample([m * inverse_density for m in momentum], step + 1)
-            send_flow(step + 1)
+    background = {1: build_slots, 2: build_deposit, 3: build_fluid}
+
+    def ring_contact(k):
+        def wait():
+            background.get(k, nothing)()
+            copies_ring[k].wait_recv()
+
+        return contact(0, shapes.at[k], lower.at[k], wait)
+
+    touch = ring_contact(0)
+    all_bytes(flow_in.at[0], flow_recv.at[0])
+    predicted = shapes[0] + time_step * vertex_flow(0, 0)
+    for k in range(ITERS):
+        (shape,) = relax([(shapes[k], predicted, touch)])
+        shapes[k + 1] = shape
+        if k < ITERS - 1:
+            copies_ring[k + 1] = send_ring(k + 1)
+            touch = ring_contact(k + 1)
+    send_force(predicted, shape, 0)
+    near_copies = [
+        remote(shapes.at[ITERS], shapes_near.at[e - 1], near_send.at[e - 1], near_recv.at[e - 1], 0, e)
+        for e in range(1, depth + 1)
+    ]
+    build_ghosts()
+    gather_force(0)
+    for q in range(3 * part // 8):
+        rows = slice(8 * q, 8 * q + 8)
+        after = collide([fluid[i, rows, :] for i in range(DIRS)], [field[c, rows, :] for c in range(3)])
+        for i in range(DIRS):
+            post[i, rows, :] = roll_z(after[i], i)
+    for i in range(DIRS):
+        step_x, step_y, _ = velocities[i]
+        for x in range(cx + 2):
+            at = (x + 1 - step_x) * long_y + 1 - step_y
+            fluid_2[i, x * short_y : (x + 1) * short_y, :] = post[i, at : at + short_y, :]
+    lines_own = [
+        jnp.concatenate(
+            [fluid_2[i, (x + 1) * short_y + 1 : (x + 1) * short_y + 1 + cy, :] for x in range(cx)], axis=0
+        )
+        for i in range(DIRS)
+    ]
+    density, momentum = moments(lines_own)
+    inverse_density = 1.0 / density
+    sample([m * inverse_density for m in momentum], 1)
+    send_flow(1)
+
+    for copy in near_copies:
+        copy.wait_recv()
+    level = [shapes.at[ITERS]] + [shapes_near.at[e - 1] for e in range(1, depth + 1)]
+    touches = [contact(e, level[e], level[e + 1], nothing) for e in range(depth)]
+    all_bytes(flow_in.at[1], flow_recv.at[1])
+    for e in range(depth):
+        predicted_of[e] = level[e][...] + time_step * vertex_flow(1, e)
+    for sweep in range(ITERS):
+        count = ITERS - sweep
+        made = relax([(level[e][...], predicted_of[e], touches[e]) for e in range(count)])
+        for e in range(count):
+            ghosts[sweep, e] = made[e]
+        level = [ghosts.at[sweep, e] for e in range(count)]
+        touches = [contact(e, level[e], level[e + 1], nothing) for e in range(count - 1)]
+    send_force(predicted_of[0], made[0], 1)
 
     for b in range(bodies):
         for c in range(3):
             r = b * BODY_ROWS + c
-            outp_ref[c, b : b + 1, :] = shapes[k, r : r + 1, 0:verts]
-    gather_force(STEPS - 1)
+            outp_ref[c, b : b + 1, :] = ghosts[ITERS - 1, 0, r : r + 1, 0:verts]
+    gather_force(1)
     for c in range(3):
         for x in range(cx + 2):
             at = (x + 1) * long_y + 1
@@ -576,7 +655,7 @@
 
     for copy in copies_ring.values():
         copy.wait_send()
-    for copy in cells_copies + edge_copies + block_copies:
+    for copy in cells_copies + edge_copies + block_copies + ghost_copies + near_copies:
         copy.wait_send()
     for step in range(STEPS):
         all_bytes(flow_out.at[step, pl.ds(0, n_brick - 1)], flow_send.at[step])
@@ -597,7 +676,6 @@
     wide = n_brick * GROUP
     long_rows = 3 * cx * (cy + 2 * RING)
     short_rows = (cx + 2) * (cy + 2)
-    sweeps = STEPS * ITERS
     blocks_v = width // LANES
     f32, bf16, i32 = jnp.float32, jnp.bfloat16, jnp.int32
     vmem = pltpu.VMEM
@@ -609,26 +687,38 @@
             jax.ShapeDtypeStruct(populations.shape, f32),
             jax.ShapeDtypeStruct(positions.shape, f32),
         ),
-        in_specs=[in_vmem, in_vmem, in_vmem, pl.BlockSpec(memory_space=pl.ANY)] + [in_vmem] * 4,
+        in_specs=[pl.BlockSpec(memory_space=pl.ANY)] * 8,
         out_specs=(in_vmem, in_vmem),
         scratch_shapes=[
+            vmem(populations.shape, f32),
+            vmem(positions.shape, f32),
+            vmem(rest_shape.shape, f32),
+            vmem(sample_cells.shape, i32),
+            vmem(vertex_slots.shape, i32),
+            vmem((2, tiles, LANES), i32),
             vmem((verts, verts), f32),
             vmem((32, width), f32),
             vmem((width, width), bf16),
             vmem((width, width), bf16),
-            vmem((tiles * LANES, LANES), bf16),
-            vmem((tiles, blocks_v * rows, LANES), bf16),
-            vmem((2 * blocks_v * rows, tiles * LANES), bf16),
-            vmem((rows * tiles, LANES), f32),
+            vmem((ITERS, 4, tiles, LANES), i32),
+            vmem((ITERS, tiles * LANES, LANES), bf16),
+            vmem((ITERS, tiles, blocks_v * rows, LANES), bf16),
+            vmem((ITERS, 2 * blocks_v * rows, tiles * LANES), bf16),
+            vmem((ITERS, rows * tiles, LANES), f32),
             vmem((bodies, width, wide), bf16),
             vmem((3, wide, LANES), bf16),
             vmem((3, 8, wide), i32),
-            vmem((LANES, LANES), f32),
-            vmem((sweeps + 1, rows, width), f32),
-            vmem((sweeps, rows, width), f32),
+            vmem((ITERS, LANES, LANES), f32),
+            vmem((ITERS + 1, rows, width), f32),
+            vmem((ITERS, rows, width), f32),
+            vmem((ITERS, rows, width), f32),
+            vmem((ITERS - 1, 2, tiles, LANES), i32),
+            vmem((ITERS - 1,) + vertex_slots.shape, i32),
+            vmem((ITERS, ITERS, rows, width), f32),
+            vmem((ITERS, rows, width), f32),
             vmem((rows, width), f32),
-            vmem((rows, width), i32),
-            vmem((1, up(bodies * verts + width, LANES)), i32),
+            vmem((ITERS, rows, width), i32),
+            vmem((ITERS, 1, up(bodies * verts + width, LANES)), i32),
             vmem((1, up(slot_count, LANES)), i32),
             vmem((3, 3, 1, up(slot_count, LANES)), i32),
             vmem((STEPS, n_brick, 1, LANES), f32),
@@ -644,9 +734,16 @@
             vmem((dirs, short_rows, LANES), f32),
             vmem((3, long_rows, LANES), f32),
             vmem((3, short_rows, LANES), f32),
-            dma,
-            dma((sweeps,)),
-            dma((sweeps,)),
+            dma((8,)),
+            pltpu.SemaphoreType.REGULAR,
+            dma((ITERS,)),
+            dma((ITERS,)),
+            dma((ITERS,)),
+            dma((ITERS,)),
+            dma((ITERS - 1,)),
+            dma((ITERS - 1,)),
+            dma((ITERS - 1,)),
+            dma((ITERS - 1,)),
             dma((STEPS,)),
             dma((STEPS,)),
             dma((STEPS,)),

time: 48.4 us -> 43.2 us (0.89)
  Pallas kernels: 44.6 us -> 39.5 us
    pallas_call x1, Pallas kernels: 44.6 us -> 39.5 us  [on_device(): pl.pallas_call(functools.partial(step_kernel, (n_brick, n_group, verts, b...]
where the time goes in v2:
time: 43.2 us; the launch traced here: 43 us
  Pallas kernels  39.5 us (91%)
  local copies, waits for them, and re-layouts  2.92 us (7%)
  between operations  0.64 us (1%)
    pallas_call x1, Pallas kernels, on_device(): pl.pallas_call(functools.partial(step_kernel, (n_brick, n_group, verts, b...  39.5 us
    unnamed x2, local copies, waits for them, and re-layouts  2.92 us

profile of v2, /device:TPU:0, one launch (start us, length us, event | category | flops | bytes accessed | tf_op | source)
XLA Modules:
  0.0 43.0 jit_solution(13662677792411339415)
XLA Ops:
  0.6 39.5 %shard_map.95 = (f32[19,2,8,128]{3,2,1,0:T(8,128)}, f32[3,2,642]{2,1,0:T(2,128)}) custom-call(f32[19,2,8,128]{3,2,1,0:T(8,128)} %pop_hbm.1, f32[3,2,642]{2,1,0:T(2,128)} %pos_hbm.1, f32[3,642]{1,0:T(4,128)} %rest_hbm.1, f32[642,642]{1,0:T(8,128)} %inv_hbm.1, s32[1,64]{1,0:T(1,128)} %cells_hbm.1, s32[1,1284]{1,0:T(1,128)} %slots_hbm.1, s32[16,128]{1,0:T(8,128)} %bitcast.2, ...), custom_call_target="tpu_custom_call" | custom-call | tf_op jit(solution)/shard_map/pallas_call | solution.py:684
  40.1 1.6 %copy.12 = f32[19,2,8,128]{3,2,1,0:T(8,128)} copy(f32[19,2,8,128]{3,2,1,0:T(8,128)} %get-tuple-element.4) | data formatting | bytes 311296
  41.7 1.3 %copy.13 = f32[3,2,642]{2,1,0:T(2,128)} copy(f32[3,2,642]{2,1,0:T(2,128)} %get-tuple-element.5) | data formatting | bytes 30816

commit v3 on v2

--- a/solution.py
+++ b/solution.py
@@ -126,8 +126,8 @@
     sizes, pop_hbm, pos_hbm, rest_hbm, inv_hbm, cells_hbm, slots_hbm, own_hbm, far_hbm,
     outf_ref, outp_ref,
     pop_ref, pos_ref, rest_in, cells_ref, slots_ref, pairs,
-    inv_raw, inv_tail, inv_high, inv_mid, places, hot, mask, lhs, spread, slot_hot, deposit, row_id, turned,
-    shapes, lower, shapes_near, pairs_near, slots_near, ghosts, predicted_of,
+    inv_raw, inv_tail, inv_high, inv_mid, inv_last, places, hot, mask, lhs, spread, slot_hot, deposit, row_id, turned,
+    shapes, lower, under, shapes_near, pairs_near, slots_near, ghosts, predicted_of,
     rest8, slot8, slot_flat, cells_own, cells_near,
     flow_out, flow_in, force_out, force_in, blocks, edges_out, edges_in, fluid, post, fluid_2, post_2,
     field, field_2,
@@ -240,8 +240,19 @@
                 flow_send.at[step], flow_recv.at[step], 0, o,
             )
 
-    def send_ring(k):
-        return remote(shapes.at[k], lower.at[k], ring_send.at[k], ring_recv.at[k], 0, 1)
+    def send_shapes(n):
+        return [
+            remote(
+                shapes.at[2 * n], lower.at[n, e - 1], ring_send.at[n, e - 1], ring_recv.at[n, e - 1], 0, e
+            )
+            for e in (1, 2)
+        ]
+
+    def send_pairs(e):
+        return remote(pairs, pairs_near.at[e - 1], pairs_send.at[e - 1], pairs_recv.at[e - 1], 0, e)
+
+    def send_slots(e):
+        return remote(slots_ref, slots_near.at[e - 1], slots_send.at[e - 1], slots_recv.at[e - 1], 0, e)
 
     lines_own = [
         jnp.concatenate([pop_ref[i, x] for x in range(cx)], axis=0) for i in range(DIRS)
@@ -254,34 +265,10 @@
     for dg in (1, -1):
         pl.semaphore_signal(ready, inc=1, device_id=(group_at(dg), brick_at(0)), device_id_type=MESH)
     send_flow(0)
-    copies = [send_ring(0)]
-    pl.semaphore_wait(ready, 2)
-    for n, (dg, db) in enumerate([(a, b) for a in (-1, 0, 1) for b in (-1, 0, 1) if (a, b) != (0, 0)]):
-        copies.append(remote(
-            cells_own, cells_near.at[1 - dg, 1 - db], cells_send.at[n], cells_recv.at[n], dg, db
-        ))
-    cells_copies = copies[1:]
-    edge_copies = [
-        remote(
-            edges_out.at[side], edges_in.at[1 - dg, side],
-            edge_send.at[dg + 1, side], edge_recv.at[dg + 1, side], dg, 1 if side else -1,
-        )
-        for dg in (0, -1, 1)
-        for side in (0, 1)
-    ]
-    block_copies = [
-        remote(pop_ref, blocks.at[n], block_send.at[n], block_recv.at[n], dg, 0)
-        for n, dg in enumerate((1, -1))
-    ]
-
-    ghost_copies = []
-    for e in range(1, depth):
-        ghost_copies.append(remote(
-            pairs, pairs_near.at[e - 1], pairs_send.at[e - 1], pairs_recv.at[e - 1], 0, e
-        ))
-        ghost_copies.append(remote(
-            slots_ref, slots_near.at[e - 1], slots_send.at[e - 1], slots_recv.at[e - 1], 0, e
-        ))
+    start_copies = send_shapes(0)
+    ghost_copies = [send_pairs(1), send_slots(1)]
+    for e in range(2, depth):
+        ghost_copies += [send_pairs(e), send_slots(e)]
 
     def place(index):
         body = jnp.zeros(index.shape, i32)
@@ -327,34 +314,52 @@
     place_slots(0, slots_ref)
 
     def build_ghosts():
-        for copy in ghost_copies:
+        for copy in ghost_copies[2:]:
             copy.wait_recv()
-        for e in range(1, depth):
+        for e in range(2, depth):
             build_pairs(e, pairs_near.at[e - 1])
             place_slots(e, slots_near.at[e - 1])
 
     inv_copy.wait()
     chunk = 32
-    full = verts // chunk
     edge = verts // LANES * LANES
-    for ref in (inv_high, inv_mid):
-        ref[:, edge:width] = jnp.zeros((width, width - edge), bf16)
-        ref[full * chunk : width, :] = jnp.zeros((width - full * chunk, width), bf16)
+    tail = verts - edge
+    main = inv_high.shape[1]
+    inv_tail[...] = jnp.zeros(inv_tail.shape, f32)
+    inv_tail[0:tail, 0:verts] = inv_raw[edge:verts, :]
 
     def split(n, _):
         at = pl.multiple_of(n * chunk, chunk)
-        high, mid = halves(inv_raw[pl.ds(at, chunk), :])
-        inv_high[pl.ds(at, chunk), 0:verts] = high.astype(bf16)
-        inv_mid[pl.ds(at, chunk), 0:verts] = mid.astype(bf16)
+        high, mid = halves(inv_raw[pl.ds(at, chunk), 0:edge])
+        high = high.astype(bf16)
+        mid = mid.astype(bf16)
+        inv_high[pl.ds(at, chunk), :] = high[:, :main]
+        inv_mid[pl.ds(at, chunk), :] = mid[:, :main]
+        inv_last[pl.ds(at, chunk), 0 : edge - main] = high[:, main:]
+        inv_last[pl.ds(at, chunk), edge - main : 2 * (edge - main)] = mid[:, main:]
         return 0
 
-    lax.fori_loop(0, full, split, 0)
-    if verts % chunk:
-        inv_tail[...] = jnp.zeros(inv_tail.shape, f32)
-        inv_tail[0 : verts % chunk, 0:verts] = inv_raw[full * chunk : verts, :]
-        high, mid = halves(inv_tail[...])
-        inv_high[full * chunk : (full + 1) * chunk, :] = high.astype(bf16)
-        inv_mid[full * chunk : (full + 1) * chunk, :] = mid.astype(bf16)
+    lax.fori_loop(0, edge // chunk, split, 0)
+
+    pl.semaphore_wait(ready, 2)
+    cells_copies = []
+    for n, (dg, db) in enumerate([(a, b) for a in (-1, 0, 1) for b in (-1, 0, 1) if (a, b) != (0, 0)]):
+        cells_copies.append(remote(
+            cells_own, cells_near.at[1 - dg, 1 - db], cells_send.at[n], cells_recv.at[n], dg, db
+        ))
+    edge_copies = [
+        remote(
+            edges_out.at[side], edges_in.at[1 - dg, side],
+            edge_send.at[dg + 1, side], edge_recv.at[dg + 1, side], dg, 1 if side else -1,
+        )
+        for dg in (0, -1, 1)
+        for side in (0, 1)
+    ]
+    block_copies = [
+        remote(pop_ref, blocks.at[n], block_send.at[n], block_recv.at[n], dg, 0)
+        for n, dg in enumerate((1, -1))
+    ]
+
 
     def pick(ref, lane, ident):
         total = [jnp.zeros((tiles, LANES), f32)] * 3
@@ -395,8 +400,6 @@
         added = added[:half] + added[half:]
         return jnp.concatenate([added[h * rows_v : (h + 1) * rows_v] for h in range(blocks_v)], axis=1)
 
-    copies_ring = {0: copies[0]}
-
     def received(step, e):
         out = []
         per_tile = LANES // peer_cells
@@ -421,23 +424,40 @@
         return jnp.concatenate(parts, axis=1)
 
     def relax(cases):
-        high, mid = [], []
+        high, mid, ends = [], [], []
         for shape, predicted, touch in cases:
             centroid = jnp.sum(shape, axis=1, keepdims=True) * (1.0 / verts)
             rhs = mass_weight * predicted + shape_weight * (centroid + rest8[...]) + touch
-            a, b = halves(rhs)
+            a, b = halves(rhs[:, :edge])
             high.append(a)
             mid.append(b)
+            more = jnp.zeros((rows_v, edge), f32)
+            last = jnp.zeros((rows_v, LANES), f32)
+            for n in range(tail):
+                row = inv_tail[n : n + 1, :]
+                more = more + rhs[:, edge + n : edge + n + 1] * row[:, :edge]
+                value = jnp.sum(rhs * row, axis=1, keepdims=True)
+                last = jnp.where(iota((rows_v, LANES), 1) == n, value, last)
+            ends.append((more, last))
         if len(cases) % 2:
-            high.append(jnp.zeros((rows_v, width), f32))
-            mid.append(jnp.zeros((rows_v, width), f32))
+            high.append(jnp.zeros((rows_v, edge), f32))
+            mid.append(jnp.zeros((rows_v, edge), f32))
         count = len(high) * rows_v
         high = jnp.concatenate(high, axis=0).astype(bf16)
         left = jnp.concatenate([high, jnp.concatenate(mid, axis=0).astype(bf16)], axis=0)
         both = jnp.dot(left, inv_high[...], preferred_element_type=f32)
         rest = jnp.dot(high, inv_mid[...], preferred_element_type=f32)
+        final = jnp.dot(left, inv_last[...], preferred_element_type=f32)
         both = both[:count] + both[count:] + rest
-        return [both[n * rows_v : (n + 1) * rows_v] for n in range(len(cases))]
+        step = edge - main
+        final = final[:count, :step] + final[count:, :step] + final[:count, step:]
+        out = []
+        for n, (more, last) in enumerate(ends):
+            rows = slice(n * rows_v, (n + 1) * rows_v)
+            out.append(jnp.concatenate(
+                [both[rows] + more[:, :main], final[rows] + more[:, main:], last], axis=1
+            ))
+        return out
 
     def build_slots():
         column_of = []
@@ -571,30 +591,44 @@
     def nothing():
         pass
 
-    background = {1: build_slots, 2: build_deposit, 3: build_fluid}
-
-    def ring_contact(k):
-        def wait():
-            background.get(k, nothing)()
-            copies_ring[k].wait_recv()
-
-        return contact(0, shapes.at[k], lower.at[k], wait)
-
-    touch = ring_contact(0)
+    def both_contacts(own, n, before_far):
+        first_touch = contact(0, own, lower.at[n, 0], before_far)
+        return [first_touch, contact(1, lower.at[n, 0], lower.at[n, 1], nothing)]
+
+    def wait_start():
+        for copy in start_copies + ghost_copies[:2]:
+            copy.wait_recv()
+        build_pairs(1, pairs_near.at[0])
+        place_slots(1, slots_near.at[0])
+
+    def wait_middle():
+        build_slots()
+        build_deposit()
+        build_ghosts()
+        for copy in middle_copies:
+            copy.wait_recv()
+
+    touches = both_contacts(shapes.at[0], 0, wait_start)
     all_bytes(flow_in.at[0], flow_recv.at[0])
-    predicted = shapes[0] + time_step * vertex_flow(0, 0)
-    for k in range(ITERS):
-        (shape,) = relax([(shapes[k], predicted, touch)])
-        shapes[k + 1] = shape
-        if k < ITERS - 1:
-            copies_ring[k + 1] = send_ring(k + 1)
-            touch = ring_contact(k + 1)
+    predicted_of[0] = shapes[0] + time_step * vertex_flow(0, 0)
+    predicted_of[1] = lower[0, 0] + time_step * vertex_flow(0, 1)
+    for n in range(ITERS // 2):
+        if n:
+            middle_copies = send_shapes(n)
+            touches = both_contacts(shapes.at[2 * n], n, wait_middle)
+        shapes[2 * n + 1], under[n] = relax([
+            (shapes[2 * n], predicted_of[0], touches[0]), (lower[n, 0], predicted_of[1], touches[1])
+        ])
+        touch = contact(0, shapes.at[2 * n + 1], under.at[n], nothing)
+        (shape,) = relax([(shapes[2 * n + 1], predicted_of[0], touch)])
+        shapes[2 * n + 2] = shape
+    predicted = predicted_of[0]
     send_force(predicted, shape, 0)
     near_copies = [
         remote(shapes.at[ITERS], shapes_near.at[e - 1], near_send.at[e - 1], near_recv.at[e - 1], 0, e)
         for e in range(1, depth + 1)
     ]
-    build_ghosts()
+    build_fluid()
     gather_force(0)
     for q in range(3 * part // 8):
         rows = slice(8 * q, 8 * q + 8)
@@ -633,10 +667,7 @@
         touches = [contact(e, level[e], level[e + 1], nothing) for e in range(count - 1)]
     send_force(predicted_of[0], made[0], 1)
 
-    for b in range(bodies):
-        for c in range(3):
-            r = b * BODY_ROWS + c
-            outp_ref[c, b : b + 1, :] = ghosts[ITERS - 1, 0, r : r + 1, 0:verts]
+    outp_ref[...] = ghosts[ITERS - 1, 0]
     gather_force(1)
     for c in range(3):
         for x in range(cx + 2):
@@ -653,13 +684,22 @@
             at = (x + 1 - step_x) * short_y + 1 - step_y
             outf_ref[i, x] = post_2[i, at : at + cy, :]
 
-    for copy in copies_ring.values():
+    for copy in start_copies + middle_copies:
         copy.wait_send()
     for copy in cells_copies + edge_copies + block_copies + ghost_copies + near_copies:
         copy.wait_send()
     for step in range(STEPS):
         all_bytes(flow_out.at[step, pl.ds(0, n_brick - 1)], flow_send.at[step])
         all_bytes(force_in.at[step, pl.ds(0, 3 * n_brick - 1)], force_send.at[step])
+
+
+def finish_kernel(fluid_ref, rows_ref, outf_ref, outp_ref):
+    outf_ref[...] = fluid_ref[...]
+    bodies, verts = outp_ref.shape[1:]
+    for b in range(bodies):
+        for c in range(3):
+            r = b * BODY_ROWS + c
+            outp_ref[c, b : b + 1, :] = rows_ref[r : r + 1, 0:verts]
 
 
 def on_device(
@@ -677,17 +717,16 @@
     long_rows = 3 * cx * (cy + 2 * RING)
     short_rows = (cx + 2) * (cy + 2)
     blocks_v = width // LANES
+    edge = verts // LANES * LANES
+    main = edge // (2 * LANES) * (2 * LANES)
     f32, bf16, i32 = jnp.float32, jnp.bfloat16, jnp.int32
     vmem = pltpu.VMEM
     dma = pltpu.SemaphoreType.DMA
     in_vmem = pl.BlockSpec(memory_space=pltpu.VMEM)
-    return pl.pallas_call(
+    fluid, shape_rows = pl.pallas_call(
         functools.partial(step_kernel, (n_brick, n_group, verts, bodies, slot_count)),
-        out_shape=(
-            jax.ShapeDtypeStruct(populations.shape, f32),
-            jax.ShapeDtypeStruct(positions.shape, f32),
-        ),
-        in_specs=[pl.BlockSpec(memory_space=pl.ANY)] * 8,
+        out_shape=(vmem(populations.shape, f32), vmem((rows, width), f32)),
+        in_specs=[pl.BlockSpec(memory_space=pltpu.HBM)] * 8,
         out_specs=(in_vmem, in_vmem),
         scratch_shapes=[
             vmem(populations.shape, f32),
@@ -697,9 +736,10 @@
             vmem(vertex_slots.shape, i32),
             vmem((2, tiles, LANES), i32),
             vmem((verts, verts), f32),
-            vmem((32, width), f32),
-            vmem((width, width), bf16),
-            vmem((width, width), bf16),
+            vmem((up(max(verts - edge, 1), 8), width), f32),
+            vmem((edge, main), bf16),
+            vmem((edge, main), bf16),
+            vmem((edge, 2 * (edge - main)), bf16),
             vmem((ITERS, 4, tiles, LANES), i32),
             vmem((ITERS, tiles * LANES, LANES), bf16),
             vmem((ITERS, tiles, blocks_v * rows, LANES), bf16),
@@ -710,7 +750,8 @@
             vmem((3, 8, wide), i32),
             vmem((ITERS, LANES, LANES), f32),
             vmem((ITERS + 1, rows, width), f32),
-            vmem((ITERS, rows, width), f32),
+            vmem((ITERS // 2, 2, rows, width), f32),
+            vmem((ITERS // 2, rows, width), f32),
             vmem((ITERS, rows, width), f32),
             vmem((ITERS - 1, 2, tiles, LANES), i32),
             vmem((ITERS - 1,) + vertex_slots.shape, i32),
@@ -736,8 +777,8 @@
             vmem((3, short_rows, LANES), f32),
             dma((8,)),
             pltpu.SemaphoreType.REGULAR,
-            dma((ITERS,)),
-            dma((ITERS,)),
+            dma((ITERS // 2, 2)),
+            dma((ITERS // 2, 2)),
             dma((ITERS,)),
             dma((ITERS,)),
             dma((ITERS - 1,)),
@@ -756,12 +797,25 @@
             dma((2,)),
         ],
         compiler_params=pltpu.CompilerParams(
-            collective_id=0, has_side_effects=True, vmem_limit_bytes=60 * 1024 * 1024
+            collective_id=0, has_side_effects=True, vmem_limit_bytes=48 * 1024 * 1024
         ),
-    )(
-        populations, positions, rest_shape, inverse, sample_cells, vertex_slots,
-        pair_own.reshape(tiles, LANES), pair_far.reshape(tiles, LANES),
-    )
+    )(*[
+        pltpu.with_memory_space_constraint(value, pltpu.HBM)
+        for value in (
+            populations, positions, rest_shape, inverse, sample_cells, vertex_slots,
+            pair_own.reshape(tiles, LANES), pair_far.reshape(tiles, LANES),
+        )
+    ])
+    return pl.pallas_call(
+        finish_kernel,
+        out_shape=(
+            jax.ShapeDtypeStruct(populations.shape, f32),
+            jax.ShapeDtypeStruct(positions.shape, f32),
+        ),
+        in_specs=[in_vmem, in_vmem],
+        out_specs=(in_vmem, in_vmem),
+        compiler_params=pltpu.CompilerParams(vmem_limit_bytes=8 * 1024 * 1024),
+    )(fluid, shape_rows)
 
 
 def solution(mesh):

time: 43.2 us -> 36.4 us (0.84)
  Pallas kernels: 39.5 us -> 35.6 us
  local copies, waits for them, and re-layouts: 2.92 us -> 0 us
    pallas_call x1, Pallas kernels: 39.5 us -> 35 us  [on_device(): pl.pallas_call(functools.partial(step_kernel, (n_brick, n_group, verts, b...]
    unnamed x2 -> x0, local copies, waits for them, and re-layouts: 2.92 us -> none
    pallas_call x0 -> x1, Pallas kernels: none -> 0.68 us  [on_device(): pl.pallas_call(finish_kernel, out_shape=(jax.ShapeDtypeStruct(populations...]
where the time goes in v3:
time: 36.4 us; the launch traced here: 36.3 us
  Pallas kernels  35.6 us (98%)
  between operations  0.64 us (2%)
    pallas_call x1, Pallas kernels, on_device(): pl.pallas_call(functools.partial(step_kernel, (n_brick, n_group, verts, b...  35 us

profile of v3, /device:TPU:0, one launch (start us, length us, event | category | flops | bytes accessed | tf_op | source)
XLA Modules:
  0.0 36.3 jit_solution(13890751501407356763)
XLA Ops:
  0.6 35.0 %shard_map.95 = (f32[19,2,8,128]{3,2,1,0:T(8,128)S(1)}, f32[8,768]{1,0:T(8,128)S(1)}) custom-call(f32[19,2,8,128]{3,2,1,0:T(8,128)} %pop_hbm.1, f32[3,2,642]{2,1,0:T(2,128)} %pos_hbm.1, f32[3,642]{1,0:T(4,128)} %rest_hbm.1, f32[642,642]{1,0:T(8,128)} %inv_hbm.1, s32[1,64]{1,0:T(1,128)} %cells_hbm.1, s32[1,1284]{1,0:T(1,128)} %slots_hbm.1, ...), custom_call_target="tpu_custom_call" | custom-call | tf_op jit(solution)/shard_map/pallas_call | solution.py:726
  35.6 0.7 %shard_map.96 = (f32[19,2,8,128]{3,2,1,0:T(8,128)}, f32[3,2,642]{2,1,0:T(2,128)}) custom-call(f32[19,2,8,128]{3,2,1,0:T(8,128)S(1)} %get-tuple-element.4.fluid_ref, f32[8,768]{1,0:T(8,128)S(1)} %get-tuple-element.5.rows_ref), custom_call_target="tpu_custom_call" | custom-call | tf_op jit(solution)/shard_map/pallas_call | solution.py:809

commit v4 on v3

--- a/solution.py
+++ b/solution.py
@@ -115,6 +115,22 @@
     return out
 
 
+def far_dirs(sign):
+    known = [i for i in range(DIRS) if velocities[i][0] == sign]
+    return known + [velocities.index((-sign, 0, 0)), velocities.index((0, 1, 0)), velocities.index((0, 0, 1)), 0]
+
+
+def far_rows(rows, sign):
+    density, momentum = moments(rows)
+    known = far_dirs(sign)[:5]
+    ahead = functools.reduce(lambda a, b: a + b, [rows[i] for i in known])
+    back = ahead - momentum[0] if sign > 0 else ahead + momentum[0]
+    at = velocities.index
+    side = momentum[1] - (rows[at((sign, 1, 0))] - rows[at((sign, -1, 0))])
+    along = momentum[2] - (rows[at((sign, 0, 1))] - rows[at((sign, 0, -1))])
+    return [rows[i] for i in known] + [back, side, along, density - ahead - back - side - along]
+
+
 def roll_z(value, index):
     step = velocities[index][2]
     if step == 0:
@@ -129,10 +145,10 @@
     inv_raw, inv_tail, inv_high, inv_mid, inv_last, places, hot, mask, lhs, spread, slot_hot, deposit, row_id, turned,
     shapes, lower, under, shapes_near, pairs_near, slots_near, ghosts, predicted_of,
     rest8, slot8, slot_flat, cells_own, cells_near,
-    flow_out, flow_in, force_out, force_in, blocks, edges_out, edges_in, fluid, post, fluid_2, post_2,
-    field, field_2,
+    flow_out, flow_in, force_out, force_in, far_out, far_in, corner_out, corner_in, edges_out, edges_in, fluid, post, fluid_own,
+    field, field_near,
     in_sem, ready, ring_send, ring_recv, near_send, near_recv, pairs_send, pairs_recv, slots_send, slots_recv, flow_send, flow_recv, force_send, force_recv,
-    cells_send, cells_recv, edge_send, edge_recv, block_send, block_recv,
+    cells_send, cells_recv, edge_send, edge_recv, far_send, far_recv, corner_send, corner_recv,
 ):
     n_brick, n_group, verts, bodies, slot_count = sizes
     me = lax.axis_index("brick")
@@ -161,7 +177,8 @@
     def iota(shape, axis):
         return lax.broadcasted_iota(i32, shape, axis)
 
-    near = [(dg, o) for dg in (0, 1, -1) for o in range(n_brick) if (dg, o) != (0, 0)]
+    by_reach = sorted(range(n_brick), key=lambda o: -min(o, n_brick - o))
+    near = [(dg, o) for dg in (1, -1, 0) for o in by_reach if (dg, o) != (0, 0)]
     first = [(0, o) for o in range(1, n_brick)] + [(1, 0), (-1, 0)]
     barrier = pltpu.get_barrier_semaphore()
     for dg, o in first:
@@ -199,11 +216,6 @@
             rest8[r : r + 1, 0:verts] = rest_in[c : c + 1, :]
     cells_own[...] = jnp.zeros(cells_own.shape, i32)
     cells_own[:, 0:slot_count] = cells_ref[...]
-    for x in range(cx):
-        for i in range(DIRS):
-            edges_out[0, i, 2 * x : 2 * x + 2, :] = pop_ref[i, x, 0:RING, :]
-            edges_out[1, i, 2 * x : 2 * x + 2, :] = pop_ref[i, x, cy - RING : cy, :]
-
     lane8 = iota((8, LANES), 1)
     sub8 = iota((8, LANES), 0)
     in_group = lane8 % GROUP
@@ -234,7 +246,7 @@
 
     def send_flow(step):
         pltpu.make_async_copy(flow_out.at[step, me], flow_in.at[step, me], flow_recv.at[step]).start()
-        for o in range(1, n_brick):
+        for o in by_reach[:-1]:
             remote(
                 flow_out.at[step, brick_at(o)], flow_in.at[step, me],
                 flow_send.at[step], flow_recv.at[step], 0, o,
@@ -267,8 +279,47 @@
     send_flow(0)
     start_copies = send_shapes(0)
     ghost_copies = [send_pairs(1), send_slots(1)]
-    for e in range(2, depth):
-        ghost_copies += [send_pairs(e), send_slots(e)]
+    def fill_ring(step, lines):
+        for n, sign in enumerate((1, -1)):
+            close = cx - 1 if sign > 0 else 0
+            for m, value in enumerate(far_rows(lines, sign)):
+                far_out[step, n, m] = value[close * cy : (close + 1) * cy]
+                for side, y in enumerate((0, cy - 1)):
+                    corner_out[step, n, side, m] = value[close * cy + y : close * cy + y + 1]
+        for i in range(DIRS):
+            for x in range(cx):
+                for side, y in enumerate((0, cy - 1)):
+                    edges_out[step, side, i, x] = lines[i][x * cy + y : x * cy + y + 1]
+
+    def send_sides(step):
+        return [
+            remote(
+                far_out.at[step, n], far_in.at[step, n], far_send.at[step, n], far_recv.at[step, n], dg, 0
+            )
+            for n, dg in enumerate((1, -1))
+        ] + [
+            remote(
+                edges_out.at[step, side], edges_in.at[step, side],
+                edge_send.at[step, side], edge_recv.at[step, side], 0, 2 * side - 1,
+            )
+            for side in (0, 1)
+        ]
+
+    def send_corners(step):
+        return [
+            remote(
+                corner_out.at[step, n, side], corner_in.at[step, n, side],
+                corner_send.at[step, 2 * n + side], corner_recv.at[step, 2 * n + side], dg, 2 * side - 1,
+            )
+            for n, dg in enumerate((1, -1))
+            for side in (0, 1)
+        ]
+
+    lines_own = [
+        jnp.concatenate([pop_ref[i, x] for x in range(cx)], axis=0) for i in range(DIRS)
+    ]
+    fill_ring(0, lines_own)
+    rim_copies = send_sides(0)
 
     def place(index):
         body = jnp.zeros(index.shape, i32)
@@ -340,26 +391,6 @@
         return 0
 
     lax.fori_loop(0, edge // chunk, split, 0)
-
-    pl.semaphore_wait(ready, 2)
-    cells_copies = []
-    for n, (dg, db) in enumerate([(a, b) for a in (-1, 0, 1) for b in (-1, 0, 1) if (a, b) != (0, 0)]):
-        cells_copies.append(remote(
-            cells_own, cells_near.at[1 - dg, 1 - db], cells_send.at[n], cells_recv.at[n], dg, db
-        ))
-    edge_copies = [
-        remote(
-            edges_out.at[side], edges_in.at[1 - dg, side],
-            edge_send.at[dg + 1, side], edge_recv.at[dg + 1, side], dg, 1 if side else -1,
-        )
-        for dg in (0, -1, 1)
-        for side in (0, 1)
-    ]
-    block_copies = [
-        remote(pop_ref, blocks.at[n], block_send.at[n], block_recv.at[n], dg, 0)
-        for n, dg in enumerate((1, -1))
-    ]
-
 
     def pick(ref, lane, ident):
         total = [jnp.zeros((tiles, LANES), f32)] * 3
@@ -515,17 +546,44 @@
                     column == lane_square, 1.0, 0.0
                 ).astype(bf16)
 
-    def build_fluid():
-        for copy in edge_copies + block_copies:
+    def build_fluid(step, own, copies):
+        for copy in copies:
             copy.wait_recv()
+
+        def put(i, plane, middle, lower_end, upper_end):
+            at = plane * short_y
+            fluid[i, at + 1 : at + 1 + cy, :] = middle
+            fluid[i, at : at + 1, :] = lower_end
+            fluid[i, at + 1 + cy : at + short_y, :] = upper_end
+
         for i in range(DIRS):
-            for dg in range(3):
-                source = pop_ref if dg == 1 else blocks.at[0 if dg == 0 else 1]
-                for x in range(cx):
-                    at = (dg * cx + x) * long_y
-                    fluid[i, at + RING : at + RING + cy, :] = source[i, x]
-                    fluid[i, at + RING + cy : at + long_y, :] = edges_in[dg, 0, i, 2 * x : 2 * x + 2, :]
-                    fluid[i, at : at + RING, :] = edges_in[dg, 1, i, 2 * x : 2 * x + 2, :]
+            for x in range(cx):
+                put(i, x + 1, own[i, x], edges_in[step, 1, i, x], edges_in[step, 0, i, x])
+            for n, (plane, sign) in enumerate(((0, 1), (cx + 1, -1))):
+                kept = far_dirs(sign)
+                if i in kept:
+                    m = kept.index(i)
+                    put(i, plane, far_in[step, n, m], corner_in[step, n, 1, m], corner_in[step, n, 0, m])
+                else:
+                    fluid[i, plane * short_y : (plane + 1) * short_y, :] = jnp.zeros((short_y, LANES), f32)
+
+    def advance(target):
+        for c in range(3):
+            for x in range(cx + 2):
+                at = (x + 1) * long_y + 1
+                field_near[c, x * short_y : (x + 1) * short_y, :] = field[c, at : at + short_y, :]
+        for q in range((cx + 2) * short_y // 8):
+            rows = slice(8 * q, 8 * q + 8)
+            after = collide(
+                [fluid[i, rows, :] for i in range(DIRS)], [field_near[c, rows, :] for c in range(3)]
+            )
+            for i in range(DIRS):
+                post[i, rows, :] = roll_z(after[i], i)
+        for i in range(DIRS):
+            step_x, step_y, _ = velocities[i]
+            for x in range(cx):
+                at = (x + 1 - step_x) * short_y + 1 - step_y
+                target[i, x] = post[i, at : at + cy, :]
 
     def send_force(predicted, shape, step):
         change = coupling_gain * (shape - predicted)
@@ -591,31 +649,43 @@
     def nothing():
         pass
 
-    def both_contacts(own, n, before_far):
+    def both_contacts(own, n, before_far, between):
         first_touch = contact(0, own, lower.at[n, 0], before_far)
+        between()
         return [first_touch, contact(1, lower.at[n, 0], lower.at[n, 1], nothing)]
 
     def wait_start():
-        for copy in start_copies + ghost_copies[:2]:
+        start_copies[0].wait_recv()
+
+    def wait_under():
+        for copy in ghost_copies[:2]:
             copy.wait_recv()
         build_pairs(1, pairs_near.at[0])
         place_slots(1, slots_near.at[0])
+        start_copies[1].wait_recv()
 
     def wait_middle():
         build_slots()
-        build_deposit()
-        build_ghosts()
         for copy in middle_copies:
             copy.wait_recv()
 
-    touches = both_contacts(shapes.at[0], 0, wait_start)
+    touches = both_contacts(shapes.at[0], 0, wait_start, wait_under)
+    pl.semaphore_wait(ready, 2)
+    cells_copies = []
+    for n, (dg, db) in enumerate([(a, b) for a in (-1, 0, 1) for b in (-1, 0, 1) if (a, b) != (0, 0)]):
+        cells_copies.append(remote(
+            cells_own, cells_near.at[1 - dg, 1 - db], cells_send.at[n], cells_recv.at[n], dg, db
+        ))
+    rim_copies += send_corners(0)
     all_bytes(flow_in.at[0], flow_recv.at[0])
     predicted_of[0] = shapes[0] + time_step * vertex_flow(0, 0)
     predicted_of[1] = lower[0, 0] + time_step * vertex_flow(0, 1)
     for n in range(ITERS // 2):
         if n:
             middle_copies = send_shapes(n)
-            touches = both_contacts(shapes.at[2 * n], n, wait_middle)
+            for e in range(2, depth):
+                ghost_copies.extend([send_pairs(e), send_slots(e)])
+            touches = both_contacts(shapes.at[2 * n], n, wait_middle, nothing)
         shapes[2 * n + 1], under[n] = relax([
             (shapes[2 * n], predicted_of[0], touches[0]), (lower[n, 0], predicted_of[1], touches[1])
         ])
@@ -628,28 +698,20 @@
         remote(shapes.at[ITERS], shapes_near.at[e - 1], near_send.at[e - 1], near_recv.at[e - 1], 0, e)
         for e in range(1, depth + 1)
     ]
-    build_fluid()
+    build_ghosts()
+    build_deposit()
+    build_fluid(0, pop_ref, rim_copies)
     gather_force(0)
-    for q in range(3 * part // 8):
-        rows = slice(8 * q, 8 * q + 8)
-        after = collide([fluid[i, rows, :] for i in range(DIRS)], [field[c, rows, :] for c in range(3)])
-        for i in range(DIRS):
-            post[i, rows, :] = roll_z(after[i], i)
-    for i in range(DIRS):
-        step_x, step_y, _ = velocities[i]
-        for x in range(cx + 2):
-            at = (x + 1 - step_x) * long_y + 1 - step_y
-            fluid_2[i, x * short_y : (x + 1) * short_y, :] = post[i, at : at + short_y, :]
+    advance(fluid_own)
     lines_own = [
-        jnp.concatenate(
-            [fluid_2[i, (x + 1) * short_y + 1 : (x + 1) * short_y + 1 + cy, :] for x in range(cx)], axis=0
-        )
-        for i in range(DIRS)
+        jnp.concatenate([fluid_own[i, x] for x in range(cx)], axis=0) for i in range(DIRS)
     ]
     density, momentum = moments(lines_own)
     inverse_density = 1.0 / density
     sample([m * inverse_density for m in momentum], 1)
     send_flow(1)
+    fill_ring(1, lines_own)
+    last_copies = send_sides(1) + send_corners(1)
 
     for copy in near_copies:
         copy.wait_recv()
@@ -668,25 +730,13 @@
     send_force(predicted_of[0], made[0], 1)
 
     outp_ref[...] = ghosts[ITERS - 1, 0]
+    build_fluid(1, fluid_own, last_copies)
     gather_force(1)
-    for c in range(3):
-        for x in range(cx + 2):
-            at = (x + 1) * long_y + 1
-            field_2[c, x * short_y : (x + 1) * short_y, :] = field[c, at : at + short_y, :]
-    for q in range((cx + 2) * short_y // 8):
-        rows = slice(8 * q, 8 * q + 8)
-        after = collide([fluid_2[i, rows, :] for i in range(DIRS)], [field_2[c, rows, :] for c in range(3)])
-        for i in range(DIRS):
-            post_2[i, rows, :] = roll_z(after[i], i)
-    for i in range(DIRS):
-        step_x, step_y, _ = velocities[i]
-        for x in range(cx):
-            at = (x + 1 - step_x) * short_y + 1 - step_y
-            outf_ref[i, x] = post_2[i, at : at + cy, :]
+    advance(outf_ref)
 
     for copy in start_copies + middle_copies:
         copy.wait_send()
-    for copy in cells_copies + edge_copies + block_copies + ghost_copies + near_copies:
+    for copy in cells_copies + rim_copies + last_copies + ghost_copies + near_copies:
         copy.wait_send()
     for step in range(STEPS):
         all_bytes(flow_out.at[step, pl.ds(0, n_brick - 1)], flow_send.at[step])
@@ -766,13 +816,15 @@
             vmem((STEPS, n_brick, 1, LANES), f32),
             vmem((STEPS, n_brick, 1, LANES), f32),
             vmem((STEPS, 3 * n_brick, 1, LANES), f32),
-            vmem((2,) + populations.shape, f32),
-            vmem((2, dirs, 2 * cx, LANES), f32),
-            vmem((3, 2, dirs, 2 * cx, LANES), f32),
-            vmem((dirs, long_rows, LANES), f32),
-            vmem((dirs, long_rows, LANES), f32),
+            vmem((STEPS, 2, 9, cy, LANES), f32),
+            vmem((STEPS, 2, 9, cy, LANES), f32),
+            vmem((STEPS, 2, 2, 9, 1, LANES), f32),
+            vmem((STEPS, 2, 2, 9, 1, LANES), f32),
+            vmem((STEPS, 2, dirs, cx, 1, LANES), f32),
+            vmem((STEPS, 2, dirs, cx, 1, LANES), f32),
             vmem((dirs, short_rows, LANES), f32),
             vmem((dirs, short_rows, LANES), f32),
+            vmem(populations.shape, f32),
             vmem((3, long_rows, LANES), f32),
             vmem((3, short_rows, LANES), f32),
             dma((8,)),
@@ -791,10 +843,12 @@
             dma((STEPS,)),
             dma((8,)),
             dma((8,)),
-            dma((3, 2)),
-            dma((3, 2)),
-            dma((2,)),
-            dma((2,)),
+            dma((STEPS, 2)),
+            dma((STEPS, 2)),
+            dma((STEPS, 2)),
+            dma((STEPS, 2)),
+            dma((STEPS, 4)),
+            dma((STEPS, 4)),
         ],
         compiler_params=pltpu.CompilerParams(
             collective_id=0, has_side_effects=True, vmem_limit_bytes=48 * 1024 * 1024

time: 36.4 us -> 35.7 us (0.981)
  Pallas kernels: 35.6 us -> 34.9 us
    pallas_call x1, Pallas kernels: 35 us -> 34.2 us  [on_device(): pl.pallas_call(functools.partial(step_kernel, (n_brick, n_group, verts, b...]
where the time goes in v4:
time: 35.7 us; the launch traced here: 35.5 us
  Pallas kernels  34.9 us (98%)
  between operations  0.64 us (2%)
    pallas_call x1, Pallas kernels, on_device(): pl.pallas_call(functools.partial(step_kernel, (n_brick, n_group, verts, b...  34.2 us

profile of v4, /device:TPU:0, one launch (start us, length us, event | category | flops | bytes accessed | tf_op | source)
XLA Modules:
  0.0 35.5 jit_solution(9234480975324858251)
XLA Ops:
  0.6 34.2 %shard_map.95 = (f32[19,2,8,128]{3,2,1,0:T(8,128)S(1)}, f32[8,768]{1,0:T(8,128)S(1)}) custom-call(f32[19,2,8,128]{3,2,1,0:T(8,128)} %pop_hbm.1, f32[3,2,642]{2,1,0:T(2,128)} %pos_hbm.1, f32[3,642]{1,0:T(4,128)} %rest_hbm.1, f32[642,642]{1,0:T(8,128)} %inv_hbm.1, s32[1,64]{1,0:T(1,128)} %cells_hbm.1, s32[1,1284]{1,0:T(1,128)} %slots_hbm.1, ...), custom_call_target="tpu_custom_call" | custom-call | tf_op jit(solution)/shard_map/pallas_call | solution.py:776
  34.8 0.7 %shard_map.96 = (f32[19,2,8,128]{3,2,1,0:T(8,128)}, f32[3,2,642]{2,1,0:T(2,128)}) custom-call(f32[19,2,8,128]{3,2,1,0:T(8,128)S(1)} %get-tuple-element.4.fluid_ref, f32[8,768]{1,0:T(8,128)S(1)} %get-tuple-element.5.rows_ref), custom_call_target="tpu_custom_call" | custom-call | tf_op jit(solution)/shard_map/pallas_call | solution.py:863

commit v5 on v4

--- a/solution.py
+++ b/solution.py
@@ -257,7 +257,7 @@
             remote(
                 shapes.at[2 * n], lower.at[n, e - 1], ring_send.at[n, e - 1], ring_recv.at[n, e - 1], 0, e
             )
-            for e in (1, 2)
+            for e in ((2, 1) if n else (1, 2))
         ]
 
     def send_pairs(e):
@@ -677,14 +677,14 @@
             cells_own, cells_near.at[1 - dg, 1 - db], cells_send.at[n], cells_recv.at[n], dg, db
         ))
     rim_copies += send_corners(0)
+    for e in range(2, depth):
+        ghost_copies += [send_pairs(e), send_slots(e)]
     all_bytes(flow_in.at[0], flow_recv.at[0])
     predicted_of[0] = shapes[0] + time_step * vertex_flow(0, 0)
     predicted_of[1] = lower[0, 0] + time_step * vertex_flow(0, 1)
     for n in range(ITERS // 2):
         if n:
             middle_copies = send_shapes(n)
-            for e in range(2, depth):
-                ghost_copies.extend([send_pairs(e), send_slots(e)])
             touches = both_contacts(shapes.at[2 * n], n, wait_middle, nothing)
         shapes[2 * n + 1], under[n] = relax([
             (shapes[2 * n], predicted_of[0], touches[0]), (lower[n, 0], predicted_of[1], touches[1])

time: 35.7 us -> 35.7 us (level)
  no operation moved by 1% of the time
where the time goes in v5:
time: 35.7 us; the launch traced here: 35.5 us
  Pallas kernels  34.9 us (98%)
  between operations  0.64 us (2%)
    pallas_call x1, Pallas kernels, on_device(): pl.pallas_call(functools.partial(step_kernel, (n_brick, n_group, verts, b...  34.2 us

profile of v5, /device:TPU:0, one launch (start us, length us, event | category | flops | bytes accessed | tf_op | source)
XLA Modules:
  0.0 35.5 jit_solution(17819365729009877890)
XLA Ops:
  0.6 34.2 %shard_map.95 = (f32[19,2,8,128]{3,2,1,0:T(8,128)S(1)}, f32[8,768]{1,0:T(8,128)S(1)}) custom-call(f32[19,2,8,128]{3,2,1,0:T(8,128)} %pop_hbm.1, f32[3,2,642]{2,1,0:T(2,128)} %pos_hbm.1, f32[3,642]{1,0:T(4,128)} %rest_hbm.1, f32[642,642]{1,0:T(8,128)} %inv_hbm.1, s32[1,64]{1,0:T(1,128)} %cells_hbm.1, s32[1,1284]{1,0:T(1,128)} %slots_hbm.1, ...), custom_call_target="tpu_custom_call" | custom-call | tf_op jit(solution)/shard_map/pallas_call | solution.py:776
  34.9 0.7 %shard_map.96 = (f32[19,2,8,128]{3,2,1,0:T(8,128)}, f32[3,2,642]{2,1,0:T(2,128)}) custom-call(f32[19,2,8,128]{3,2,1,0:T(8,128)S(1)} %get-tuple-element.4.fluid_ref, f32[8,768]{1,0:T(8,128)S(1)} %get-tuple-element.5.rows_ref), custom_call_target="tpu_custom_call" | custom-call | tf_op jit(solution)/shard_map/pallas_call | solution.py:863
